TPU v7x, 32 devices: a whole 2x2x4 slice. The times are simulated.
32 devices in a mesh: groups: 2 (over x), ctx: 4 (over y, core), heads: 4 (over z).
Axes of the slice: x: 2, y: 2, z: 4, core: 2. Of those that a mesh axis runs over, the one named last changes fastest.
Arguments:
- tokens: bfloat16 [4096, 2048], P(('groups', 'ctx', 'heads')), parts along dimension 0, may hold values from -60 to 60
- state_in: float32 [4, 256, 128], P('heads', 'groups'), parts along dimension 1, may hold values from -256 to 256
- past_kv: bfloat16 [2, 1024, 512], P(None, 'groups', 'heads'), parts along dimension 1, may hold values from -6 to 6
- w_qkv: bfloat16 [2048, 3, 512], P(None, None, 'heads'), may hold values from -0.125 to 0.125
- w_out: bfloat16 [512, 2048], P('heads'), may hold values from -0.25 to 0.25
- w_gate: bfloat16 [16, 2048, 768], P(('ctx', 'heads')), may hold values from -0.125 to 0.125
- w_up: bfloat16 [16, 2048, 768], P(('ctx', 'heads')), may hold values from -0.125 to 0.125
- w_down: bfloat16 [16, 768, 2048], P(('ctx', 'heads')), may hold values from -0.21875 to 0.21875
- expert_ids: int32 [4096, 8], P(('groups', 'ctx', 'heads')), parts along dimension 0, may hold values from 0 to 15, all different within a row; in each aligned block of 128 rows (0 to 127, 128 to 255, ...) at most 128 rows name the same one
- gate_weights: float32 [4096, 8], P(('groups', 'ctx', 'heads')), parts along dimension 0, may hold values from 0.1 to 1
Outputs:
- mixed: bfloat16 [4096, 2048], P(('groups', 'ctx', 'heads')), parts along dimension 0
There are 2 independent parts, one for each index of `groups`. A program takes and returns all parts, laid end to end along the dimension named above; an argument that names none is the same for every part. Nothing has to cross between parts.
Inputs may be any that keep to these rules, and one draw needn't show every extreme that they name: `expert_ids`: each row names 8 different experts; in each aligned block of 128 rows (the rows of one device) no expert is named by more than 128 rows, a bound that some block reaches.
All inputs are finite; a program needn't handle non-finite values.
Results may differ from a plain program's by a relative error of at most 0.017.
Values may be sent and summed in bfloat16 or wider, within the bound.
A program may use at most 128 MiB of HBM per device.

v0:
```python
import functools
import math

import jax
import jax.numpy as jnp
from jax import lax
from jax.experimental import pallas as pl
from jax.experimental.pallas import tpu as pltpu
from jax.sharding import PartitionSpec as P

HDIM = 128
WINDOW = 512


def entering(x, axis, join, neutral):
    place = lax.axis_index(axis)
    gathered = lax.all_gather(x.astype(jnp.bfloat16), axis)
    state = jnp.zeros_like(x) + jnp.asarray(neutral, x.dtype)

    def one(lap, state):
        return join(state, lax.dynamic_index_in_dim(gathered, lap, 0, False).astype(x.dtype))

    return lax.fori_loop(0, place, one, state)


def from_behind(block, axis, distance):
    devices = range(lax.axis_size(axis))
    route = [(i - distance, i) for i in devices if i - distance in devices]
    return lax.ppermute(block, axis, route)


def normalize(value):
    return value * lax.rsqrt(jnp.mean(value * value, axis=-1, keepdims=True) + 1e-06)


MESH = pl.DeviceIdType.MESH
VMEM_BYTES = 60 * 1024 * 1024
ADD_ROWS = 16
DOT_COLUMNS = 512
LAG = 2


def place(count):
    z = lax.axis_index("heads")
    c = lax.axis_index("ctx")
    beside = c + 1 - 2 * lax.rem(c, 2)
    across = lax.rem(c + 2, 4)
    diagonal = lax.rem(beside + 2, 4)
    return z, c, beside, across, diagonal


def greet(z, count, beside, across):
    barrier = pltpu.get_barrier_semaphore()

    def signal(target):
        pl.semaphore_signal(barrier, inc=1, device_id=target, device_id_type=MESH)

    signal({"ctx": beside})
    signal({"ctx": across})

    @pl.when(z > 0)
    def _():
        signal({"heads": z - 1})

    @pl.when(z < count - 1)
    def _():
        signal({"heads": z + 1})

    pl.semaphore_wait(barrier, 2 + jnp.minimum(z, 1) + jnp.minimum(count - 1 - z, 1))


def gather_kernel(count, kinds, *refs):
    size = len(kinds)
    groups = [refs[first * size : (first + 1) * size] for first in range(4)]
    own_sem = refs[4 * size]
    z, c, beside, across, diagonal = place(count)
    greet(z, count, beside, across)

    def origin(kind, source, full):
        if kind != "share":
            return source
        share = full.shape[1]
        return source.at[pl.ds(pl.multiple_of(c * share, share), share), :]

    def slot_of(kind, zz, cc):
        return {"group": cc * count + zz, "share": zz * 4 + cc, "line": zz}[kind]

    def copies(zz, cc, way, target, own=False):
        result = []
        for kind, source, full, send, recv in zip(kinds, *groups):
            if kind == "line" and (way > 1 or cc is not c):
                continue
            slot = slot_of(kind, zz, cc)
            result.append(
                pltpu.make_async_remote_copy(
                    src_ref=origin(kind, source, full) if own else full.at[slot],
                    dst_ref=full.at[slot],
                    send_sem=send.at[way, slot],
                    recv_sem=recv.at[slot],
                    device_id=target,
                    device_id_type=MESH,
                )
            )
        return result

    def start(zz, cc, way, target, own=False):
        for copy in copies(zz, cc, way, target, own):
            copy.start()

    def arrived(zz, cc):
        for copy in copies(zz, cc, 0, {"ctx": beside}):
            copy.wait_recv()

    def left(zz, cc, way, target):
        for copy in copies(zz, cc, way, target):
            copy.wait_send()

    def along(act, down, up, zz, **options):
        if down:

            @pl.when(z > 0)
            def _():
                act(zz, c, 0, {"heads": z - 1}, **options)

        if up:

            @pl.when(z < count - 1)
            def _():
                act(zz, c, 1, {"heads": z + 1}, **options)

        act(zz, c, 2, {"ctx": across}, **options)
        act(zz, c, 3, {"ctx": beside}, **options)

    local = [
        pltpu.make_async_copy(
            origin(kind, source, full), full.at[slot_of(kind, z, c)], own_sem.at[index]
        )
        for index, (kind, source, full) in enumerate(zip(kinds, *groups[:2]))
    ]
    for copy in local:
        copy.start()
    along(start, True, True, z, own=True)

    def over(zz):
        arrived(zz, across)
        start(zz, across, 3, {"ctx": beside})

    for d in range(1, count + 1):
        if d < count:

            @pl.when(z >= d)
            def _():
                arrived(z - d, c)
                along(start, False, True, z - d)

            @pl.when(z + d < count)
            def _():
                arrived(z + d, c)
                along(start, True, False, z + d)

        if d == 1:
            over(z)
        else:

            @pl.when(z >= d - 1)
            def _():
                over(z - d + 1)

            @pl.when(z + d - 1 < count)
            def _():
                over(z + d - 1)

    for zz in range(count):
        arrived(zz, beside)
        arrived(zz, diagonal)
    for copy in local:
        copy.wait()
    along(left, True, True, z)
    for d in range(1, count):

        @pl.when(z >= d)
        def _():
            along(left, False, True, z - d)

        @pl.when(z + d < count)
        def _():
            along(left, True, False, z + d)

    for zz in range(count):
        left(zz, across, 3, {"ctx": beside})


def scatter_kernel(
    count, hid_ref, down_ref, weight_ref, out_ref, part_ref, from_beside, from_across, below, above, to_across, to_line,
    beside_send, beside_recv, across_send, across_recv, line_send, below_recv, above_recv,
):
    z, c, beside, across, diagonal = place(count)
    greet(z, count, beside, across)

    def nth(index):
        more = jnp.maximum(z, count - 1 - z)
        fewer = count - 1 - more
        alone = more - fewer
        paired = jnp.maximum(index - alone, 0)
        up = jnp.where(z + more < count, more - index, index - more)
        both = (fewer - paired // 2) * (1 - 2 * (paired % 2))
        offset = jnp.where(index < alone, up, both)
        return z + jnp.where(index < count - 1, offset, 0)

    def compute(slot):
        weight = weight_ref[slot][:, :1]

        def tile(index, _):
            columns = pl.ds(pl.multiple_of(index * DOT_COLUMNS, DOT_COLUMNS), DOT_COLUMNS)
            product = jnp.dot(
                hid_ref[slot], down_ref[:, columns], preferred_element_type=jnp.float32
            )
            part_ref[slot, :, columns] = (weight * product).astype(part_ref.dtype)
            return 0

        lax.fori_loop(0, down_ref.shape[1] // DOT_COLUMNS, tile, 0)

    def beside_copy(kind, zz):
        cc = diagonal if kind == 0 else beside
        return pltpu.make_async_remote_copy(
            src_ref=part_ref.at[cc * count + zz],
            dst_ref=from_beside.at[kind, zz],
            send_sem=beside_send.at[kind, zz],
            recv_sem=beside_recv.at[kind, zz],
            device_id={"ctx": beside},
            device_id_type=MESH,
        )

    def across_copy(zz):
        return pltpu.make_async_remote_copy(
            src_ref=to_across.at[zz],
            dst_ref=from_across.at[zz],
            send_sem=across_send.at[zz],
            recv_sem=across_recv.at[zz],
            device_id={"ctx": across},
            device_id_type=MESH,
        )

    def up_copy(zz):
        return pltpu.make_async_remote_copy(
            src_ref=to_line.at[zz],
            dst_ref=below.at[zz],
            send_sem=line_send.at[zz],
            recv_sem=below_recv.at[zz],
            device_id={"heads": z + 1},
            device_id_type=MESH,
        )

    def down_copy(zz):
        return pltpu.make_async_remote_copy(
            src_ref=to_line.at[zz],
            dst_ref=above.at[zz],
            send_sem=line_send.at[zz],
            recv_sem=above_recv.at[zz],
            device_id={"heads": z - 1},
            device_id_type=MESH,
        )

    def add(target, sources):
        def chunk(index, _):
            rows = pl.ds(pl.multiple_of(index * ADD_ROWS, ADD_ROWS), ADD_ROWS)
            total = sources[0][rows, :].astype(jnp.float32)
            for source in sources[1:]:
                total = total + source[rows, :].astype(jnp.float32)
            target[rows, :] = total.astype(target.dtype)
            return 0

        lax.fori_loop(0, target.shape[0] // ADD_ROWS, chunk, 0)

    def project(zz):
        compute(diagonal * count + zz)
        beside_copy(0, zz).start()
        compute(across * count + zz)
        beside_copy(0, zz).wait_recv()
        add(to_across.at[zz], [part_ref.at[across * count + zz], from_beside.at[0, zz]])
        across_copy(zz).start()
        compute(beside * count + zz)
        beside_copy(1, zz).start()
        compute(c * count + zz)

    def onward(zz, copy, arriving, first, sources):
        @pl.when(first)
        def _():
            add(to_line.at[zz], sources)

        @pl.when(jnp.logical_not(first))
        def _():
            copy(zz).wait_recv()
            add(to_line.at[zz], sources + [arriving.at[zz]])

        copy(zz).start()

    def pass_line(zz):
        beside_copy(1, zz).wait_recv()
        across_copy(zz).wait_recv()
        sources = [part_ref.at[c * count + zz], from_beside.at[1, zz], from_across.at[zz]]

        @pl.when(zz > z)
        def _():
            onward(zz, up_copy, below, z == 0, sources)

        @pl.when(zz < z)
        def _():
            onward(zz, down_copy, above, z == count - 1, sources)

        @pl.when(zz == z)
        def _():
            add(out_ref, sources)

            @pl.when(z > 0)
            def _():
                up_copy(zz).wait_recv()
                add(out_ref, [out_ref, below.at[zz]])

            @pl.when(z < count - 1)
            def _():
                down_copy(zz).wait_recv()
                add(out_ref, [out_ref, above.at[zz]])

    def step(index, _):
        @pl.when(index < count)
        def _():
            project(nth(index))

        @pl.when(index >= LAG)
        def _():
            pass_line(nth(index - LAG))

        return 0

    lax.fori_loop(0, count + LAG, step, 0)

    for zz in range(count):
        beside_copy(0, zz).wait_send()
        beside_copy(1, zz).wait_send()
        across_copy(zz).wait_send()

        @pl.when(zz > z)
        def _():
            up_copy(zz).wait_send()

        @pl.when(zz < z)
        def _():
            down_copy(zz).wait_send()


def gather_blocks(kinds, operands, collective_id, name):
    count, ctx_count = lax.axis_size("heads"), lax.axis_size("ctx")
    slots = [count if kind == "line" else count * ctx_count for kind in kinds]
    shapes = [
        (value.shape[0] // ctx_count if kind == "share" else value.shape[0], value.shape[1])
        for kind, value in zip(kinds, operands)
    ]
    return pl.pallas_call(
        functools.partial(gather_kernel, count, kinds),
        out_shape=[
            jax.ShapeDtypeStruct((slot,) + shape, value.dtype)
            for slot, shape, value in zip(slots, shapes, operands)
        ],
        in_specs=[pl.BlockSpec(memory_space=pltpu.VMEM)] * len(kinds),
        out_specs=[pl.BlockSpec(memory_space=pl.ANY)] * len(kinds),
        scratch_shapes=[pltpu.SemaphoreType.DMA((4, slot)) for slot in slots]
        + [pltpu.SemaphoreType.DMA((slot,)) for slot in slots]
        + [pltpu.SemaphoreType.DMA((len(kinds),))],
        compiler_params=pltpu.CompilerParams(
            collective_id=collective_id, has_side_effects=True
        ),
        name=name,
    )(*operands)


def scatter_sums(hid, down, weights):
    count = lax.axis_size("heads")
    devices, rows, _ = hid.shape
    block = (rows, down.shape[1])
    dma = pltpu.SemaphoreType.DMA
    return pl.pallas_call(
        functools.partial(scatter_kernel, count),
        out_shape=jax.ShapeDtypeStruct(block, jnp.float32),
        in_specs=[pl.BlockSpec(memory_space=pltpu.VMEM)] * 3,
        out_specs=pl.BlockSpec(memory_space=pltpu.VMEM),
        scratch_shapes=[
            pltpu.VMEM((devices,) + block, hid.dtype),
            pltpu.VMEM((2, count) + block, hid.dtype),
        ]
        + [pltpu.VMEM((count,) + block, hid.dtype)] * 5
        + [dma((2, count))] * 2
        + [dma((count,))] * 5,
        compiler_params=pltpu.CompilerParams(
            collective_id=1, has_side_effects=True, vmem_limit_bytes=VMEM_BYTES
        ),
        name="scatter_sums",
    )(hid, down, weights)


def gather_inputs(tokens, w_out):
    if lax.axis_size("ctx") == 4 and w_out.shape[0] % 64 == 0:
        slab, w_rows = gather_blocks(("line", "share"), (tokens, w_out), 2, "gather_inputs")
        width = tokens.shape[1]
        return slab.reshape(-1, width), w_rows.reshape(-1, w_out.shape[1])
    return [lax.all_gather(value, "heads", axis=0, tiled=True) for value in (tokens, w_out)]


def dense_experts(
    hidden_float, normed, w_gate, w_up, w_down, expert_ids, gate_weights, expert_count
):
    axes = ("ctx", "heads")
    exp_local = w_gate.shape[0]
    chosen = expert_ids[:, :, None] == jnp.arange(expert_count, dtype=jnp.int32)
    table = jnp.sum(jnp.where(chosen, gate_weights[:, :, None], 0.0), axis=1)
    first = lax.axis_index(axes) * exp_local
    rows, tables = gather_blocks(
        ("group", "group"), (normed, table.T), 0, "gather_rows"
    )
    device_count, row_count, width = rows.shape
    rows = rows.reshape(device_count * row_count, width)
    routed = 0.0
    for e in range(exp_local):
        gate_act = jnp.dot(rows, w_gate[e], preferred_element_type=jnp.float32)
        up_act = jnp.dot(rows, w_up[e], preferred_element_type=jnp.float32)
        hid = (jax.nn.silu(gate_act) * up_act).astype(jnp.bfloat16)
        weight = lax.dynamic_index_in_dim(tables, first + e, 1, False)
        weight = jnp.broadcast_to(weight[:, :, None], (device_count, row_count, HDIM))
        hid = hid.reshape(device_count, row_count, hid.shape[1])
        routed = routed + scatter_sums(hid, w_down[e], weight)
    return (hidden_float + routed).astype(jnp.bfloat16)


def on_device(
    tokens, state_in, past_kv, w_qkv, w_out, w_gate, w_up, w_down, expert_ids, gate_weights
):
    row_count, model_width = tokens.shape
    inner_width = w_qkv.shape[2]
    local_heads = inner_width // HDIM
    w_flat = w_qkv.reshape(model_width, 3 * inner_width)
    slab, w_rows = gather_inputs(tokens, w_out)
    projected = jnp.dot(
        slab,
        w_flat,
        preferred_element_type=jnp.float32,
    ).astype(jnp.bfloat16)
    slab_rows = projected.shape[0]
    projected = projected.reshape(slab_rows, 3, local_heads, HDIM)
    query = jnp.transpose(projected[:, 0], (1, 0, 2))
    keys = jnp.transpose(projected[:, 1], (1, 0, 2))
    values = jnp.transpose(projected[:, 2], (1, 0, 2))
    local_state = jnp.einsum("hsd,hse->hde", keys, values, preferred_element_type=jnp.float32)
    earlier_state = entering(
        local_state, "ctx", lambda first, second: first + second, jnp.zeros_like(local_state)
    )
    start_state = state_in + earlier_state
    tail = jnp.stack([keys, values], axis=0)
    arrived = from_behind(tail, "ctx", 1)
    past = jnp.transpose(past_kv.reshape(2, WINDOW, local_heads, HDIM), (0, 2, 1, 3))
    previous = jnp.where(lax.axis_index("ctx") == 0, past, arrived)
    all_keys = jnp.concatenate([previous[0], keys], axis=1)
    all_values = jnp.concatenate([previous[1], values], axis=1)
    block_rows = min(slab_rows, 512)
    block_count = slab_rows // block_rows
    scale = 1.0 / math.sqrt(HDIM)
    causal = jnp.arange(block_rows)[:, None] >= jnp.arange(block_rows)[None, :]
    offsets = jnp.arange(WINDOW + block_rows)[None, :] - jnp.arange(block_rows)[:, None]
    in_window = (offsets > 0) & (offsets <= WINDOW)

    def block_step(state, index):
        first = index * block_rows
        carried = jnp.einsum(
            "hsd,hde->hse", query.astype(jnp.float32), state, precision=lax.Precision.HIGHEST
        )
        inside = jnp.einsum("hsd,htd->hst", query, keys, preferred_element_type=jnp.float32)
        inside = jnp.where(causal[None], inside, 0.0).astype(jnp.bfloat16)
        linear = carried + jnp.einsum(
            "hst,hte->hse", inside, values, preferred_element_type=jnp.float32
        )
        scores = (
            jnp.einsum("hsd,htd->hst", query, all_keys, preferred_element_type=jnp.float32) * scale
        )
        scores = jnp.where(in_window[None], scores, -jnp.inf)
        top_score = jnp.max(scores, axis=-1, keepdims=True)
        expo = jnp.exp(scores - top_score)
        probs = (expo / jnp.sum(expo, axis=-1, keepdims=True)).astype(jnp.bfloat16)
        window_out = jnp.einsum(
            "hst,hte->hse", probs, all_values, preferred_element_type=jnp.float32
        )
        combined = (normalize(linear) + window_out).astype(jnp.bfloat16)
        new_state = state + jnp.einsum(
            "hsd,hse->hde", keys, values, preferred_element_type=jnp.float32
        )
        return (new_state, combined)

    _, outs = lax.scan(block_step, start_state, jnp.arange(block_count, dtype=jnp.int32))
    heads_out = jnp.transpose(outs, (0, 2, 1, 3)).reshape(slab_rows, inner_width)
    regrouped = lax.all_to_all(heads_out, "heads", split_axis=0, concat_axis=1, tiled=True)
    attn = jnp.dot(
        regrouped,
        w_rows,
        preferred_element_type=jnp.float32,
    )
    hidden_state = (tokens.astype(jnp.float32) + attn).astype(jnp.bfloat16)
    hidden_float = hidden_state.astype(jnp.float32)
    normed = normalize(hidden_float).astype(jnp.bfloat16)
    ctx_count = lax.axis_size("ctx")
    head_count = lax.axis_size("heads")
    exp_local = w_gate.shape[0]
    expert_count = exp_local * ctx_count * head_count
    top_count = expert_ids.shape[1]
    capacity = max(2, 2 * row_count * top_count // expert_count)
    devices = ctx_count * head_count
    if ctx_count == 4 and row_count * devices <= expert_count * capacity:
        return dense_experts(
            hidden_float, normed, w_gate, w_up, w_down, expert_ids, gate_weights, expert_count
        )
    picks = expert_ids.reshape(-1)
    onehot = (picks[:, None] == jnp.arange(expert_count, dtype=jnp.int32)[None, :]).astype(
        jnp.int32
    )
    earlier = jnp.cumsum(onehot, axis=0) - onehot
    slots = jnp.sum(onehot * earlier, axis=1)
    destination = picks * capacity + slots
    source_rows = jnp.arange(row_count * top_count, dtype=jnp.int32) // top_count
    outgoing = jnp.zeros((expert_count * capacity, model_width), jnp.bfloat16)
    outgoing = outgoing.at[destination].set(normed[source_rows])
    sendable = outgoing.reshape(expert_count, 1, capacity, model_width)
    arrived_rows = lax.all_to_all(
        sendable, ("ctx", "heads"), split_axis=0, concat_axis=1, tiled=True
    )
    e_count, n_count, c_count, d_count = arrived_rows.shape
    flat = arrived_rows.reshape(e_count, n_count * c_count, d_count)
    gate_act = jnp.einsum("erd,edf->erf", flat, w_gate, preferred_element_type=jnp.float32)
    up_act = jnp.einsum("erd,edf->erf", flat, w_up, preferred_element_type=jnp.float32)
    hid = (jax.nn.silu(gate_act) * up_act).astype(jnp.bfloat16)
    out_rows = jnp.einsum("erf,efd->erd", hid, w_down, preferred_element_type=jnp.float32)
    finished = out_rows.astype(jnp.bfloat16).reshape(e_count, n_count, c_count, d_count)
    returned = lax.all_to_all(finished, ("ctx", "heads"), split_axis=1, concat_axis=0, tiled=True)
    returned = returned.reshape(expert_count * capacity, model_width)
    picked = returned[destination].reshape(row_count, top_count, model_width).astype(jnp.float32)
    routed = jnp.sum(gate_weights[:, :, None] * picked, axis=1)
    return (hidden_float + routed).astype(jnp.bfloat16)


def solution(mesh):
    return jax.shard_map(
        on_device,
        mesh=mesh,
        in_specs=(
            P(("groups", "ctx", "heads"), None),
            P("heads", "groups", None),
            P(None, "groups", "heads"),
            P(None, None, "heads"),
            P("heads", None),
            P(("ctx", "heads"), None, None),
            P(("ctx", "heads"), None, None),
            P(("ctx", "heads"), None, None),
            P(("groups", "ctx", "heads"), None),
            P(("groups", "ctx", "heads"), None),
        ),
        out_specs=P(("groups", "ctx", "heads"), None),
        check_vma=False,
    )
```

profile of v0, /device:TPU:0, one launch (start us, length us, event | category | flops | bytes accessed | tf_op | source)
XLA Modules:
  0.0 238.4 jit_solution(9478228116254334570)
XLA Ops:
  0.0 2.8 %copy.27 = bf16[2048,3,128]{0,2,1:T(8,128)(2,1)} copy(bf16[2048,3,128]{2,0,1:T(8,128)(2,1)} %param.15) | data formatting | bytes 3145728 | tf_op args[3]
  2.8 58.6 %gather_inputs.1 = (bf16[4,128,2048]{2,1,0:T(8,128)(2,1)}, bf16[16,32,2048]{2,1,0:T(8,128)(2,1)}) custom-call(bf16[128,2048]{1,0:T(8,128)(2,1)} %refs_0_.1, bf16[128,2048]{1,0:T(8,128)(2,1)} %refs_1_.1), custom_call_target="tpu_custom_call" | custom-call | tf_op jit(solution)/shard_map/gather_inputs/pallas_call | solution.py:359
  61.4 3.0 %convolution_convert_fusion = bf16[512,384]{0,1:T(8,128)(2,1)S(1)} fusion(bf16[512,2048]{1,0:T(8,128)(2,1)} %bitcast.107, bf16[2048,384]{0,1:T(8,128)(2,1)} %bitcast.89), kind=kOutput, calls=%fused_computation.18 | convolution fusion | flops 805502976 | bytes 4063232 | tf_op jit(solution)/shard_map/dot_general | solution.py:442
  65.4 1.1 copy.35
  67.2 3.0 %collective-permute-start = (bf16[2,1,512,128]{3,2,1,0:T(8,128)(2,1)}, bf16[2,1,512,128]{3,2,1,0:T(8,128)(2,1)}, u32[]{:S(2)}, u32[]{:S(2)}) collective-permute-start(bf16[2,1,512,128]{3,2,1,0:T(8,128)(2,1)} %pad_maximum_fusion), channel_id=1, source_target_pairs={{0,4},{4,8},{8,12},{1,5},{5,9},{9,13},{2,6},{6,10},{10,14},{3,7},{... | collective-permute-start | bytes 786440 | tf_op jit(solution)/shard_map/ppermute | solution.py:29
  70.2 1.8 convolution_convert_fusion.1
  71.9 5.6 %all-gather = bf16[512,128]{1,0:T(8,128)(2,1)S(1)} all-gather(bf16[128,128]{1,0:T(8,128)(2,1)} %convolution_convert_fusion.1), channel_id=2, replica_groups=mesh['groups'=2,'ctx'=4,'heads'=4] {'ctx'}, dimensions={0}, use_global_device_ids=true | all-gather | bytes 163840 | tf_op jit(solution)/shard_map/all_gather | solution.py:17
  77.6 2.0 fusion.23
  79.5 2.3 multiply_reduce_fusion.1
  81.9 1.1 bitcast_select_fusion
  83.0 1.5 fusion.35
  86.0 0.8 copy.33
  86.7 3.3 %all-to-all-start = ((bf16[4,128,128]{1,2,0:T(8,128)(2,1)}), bf16[4,128,128]{1,2,0:T(8,128)(2,1)S(1)}, u32[]{:S(2)}, u32[]{:S(2)}) async-start(bf16[4,128,128]{1,2,0:T(8,128)(2,1)} %copy.33), calls=%async_computation | async-start | bytes 262144 | tf_op jit(solution)/shard_map/all_to_all | solution.py:498
  90.7 5.9 %all-to-all-done = bf16[4,128,128]{1,2,0:T(8,128)(2,1)S(1)} async-done(((bf16[4,128,128]{1,2,0:T(8,128)(2,1)}), bf16[4,128,128]{1,2,0:T(8,128)(2,1)S(1)}, u32[]{:S(2)}, u32[]{:S(2)}) %all-to-all-start) | async-done | bytes 131104 | tf_op jit(solution)/shard_map/all_to_all | solution.py:498
  96.6 2.2 multiply_reduce_fusion
  98.8 1.0 copy-done.1
  99.9 0.9 multiply_convert_fusion.1.refs_0_
  100.8 52.7 %gather_rows.1 = (bf16[16,128,2048]{2,1,0:T(8,128)(2,1)}, f32[16,16,128]{2,1,0:T(8,128)}) custom-call(bf16[128,2048]{1,0:T(8,128)(2,1)} %multiply_convert_fusion.1.refs_0_, f32[16,128]{1,0:T(8,128)} %bitcast.103), custom_call_target="tpu_custom_call" | custom-call | tf_op jit(solution)/shard_map/gather_rows/pallas_call | solution.py:359
  153.5 9.8 %fusion.1 = f32[2048,768]{1,0:T(8,128)S(1)} fusion(bf16[2048,2048]{1,0:T(8,128)(2,1)} %bitcast.105, bf16[1,2048,768]{2,1,0:T(8,128)(2,1)S(1)} %copy-done), kind=kOutput, calls=%fused_computation.3 | convolution fusion | flops 6442450944 | bytes 17825792 | tf_op jit(solution)/shard_map/dot_general | solution.py:424
  163.4 8.5 %multiply_convert_fusion = bf16[2048,768]{1,0:T(8,128)(2,1)} fusion(f32[2048,768]{1,0:T(8,128)S(1)} %fusion.1, bf16[2048,2048]{1,0:T(8,128)(2,1)S(1)} %bitcast.106, bf16[1,2048,768]{2,1,0:T(8,128)(2,1)S(1)} %copy-done.9), kind=kOutput, calls=%fused_computation.1 | convolution fusion | flops 6451888128 | bytes 20971520 | tf_op jit(solution)/shard_map/dot_general | solution.py:425
  171.9 0.8 constant_dynamic-slice_fusion
  172.7 1.3 broadcast_in_dim.61.weight_ref
  174.1 61.9 %scatter_sums.1 = f32[128,2048]{1,0:T(8,128)} custom-call(bf16[16,128,768]{2,1,0:T(8,128)(2,1)} %bitcast.87, bf16[768,2048]{1,0:T(8,128)(2,1)} %bitcast.86, f32[16,128,128]{2,1,0:T(8,128)} %broadcast_in_dim.61.weight_ref), custom_call_target="tpu_custom_call" | custom-call | tf_op jit(solution)/shard_map/scatter_sums/pallas_call | solution.py:382
  235.9 2.5 %add_convert_fusion = bf16[128,2048]{1,0:T(8,128)(2,1)} fusion(f32[128,2048]{1,0:T(8,128)} %copy-done.1, f32[128,2048]{1,0:T(8,128)} %scatter_sums.1), kind=kLoop, calls=%fused_computation.24 | loop fusion | flops 524288 | bytes 2621440 | tf_op jit(solution)/shard_map/convert_element_type | solution.py:431
  (34 shorter events, 3.8 us)
Async XLA Ops:
  0.0 153.5 %copy-start = (bf16[1,2048,768]{2,1,0:T(8,128)(2,1)S(1)}, bf16[1,2048,768]{2,1,0:T(8,128)(2,1)}, u32[]{:S(2)}) copy-start(bf16[1,2048,768]{2,1,0:T(8,128)(2,1)} %param.17) | copy-start | bytes 9437188
  64.4 0.8 copy-start.4
  64.5 13.1 %copy-start.5 = (f32[1,128,128]{2,1,0:T(8,128)S(1)}, f32[1,128,128]{2,1,0:T(8,128)}, u32[]{:S(2)}) copy-start(f32[1,128,128]{2,1,0:T(8,128)} %param.13) | copy-start | bytes 196612
  65.4 6.6 %copy-start.2 = (bf16[512,1,1,128]{3,0,2,1:T(8,128)(2,1)}, bf16[512,1,1,128]{3,0,2,1:T(8,128)(2,1)S(1)}, u32[]{:S(2)}) copy-start(bf16[512,1,1,128]{3,0,2,1:T(8,128)(2,1)S(1)} %copy.34) | copy-start | bytes 393220
  67.2 14.7 %collective-permute-start = (bf16[2,1,512,128]{3,2,1,0:T(8,128)(2,1)}, bf16[2,1,512,128]{3,2,1,0:T(8,128)(2,1)}, u32[]{:S(2)}, u32[]{:S(2)}) collective-permute-start(bf16[2,1,512,128]{3,2,1,0:T(8,128)(2,1)} %pad_maximum_fusion), channel_id=1, source_target_pairs={{0,4},{4,8},{8,12},{1,5},{5,9},{9,13},{2,6},{6,10},{10,14},{3,7},{... | collective-permute-start | bytes 786440 | tf_op jit(solution)/shard_map/ppermute | solution.py:29
  77.6 5.4 %copy-start.3 = (bf16[512,1,1,128]{3,0,2,1:T(8,128)(2,1)S(1)}, bf16[512,1,1,128]{3,0,2,1:T(8,128)(2,1)}, u32[]{:S(2)}) copy-start(bf16[512,1,1,128]{3,0,2,1:T(8,128)(2,1)} %copy-done.2) | copy-start | bytes 393220
  84.4 1.0 copy-start.10
  85.4 4.7 %copy-start.6 = (f32[128,8]{0,1:T(8,128)S(1)}, f32[128,8]{0,1:T(8,128)}, u32[]{:S(2)}) copy-start(f32[128,8]{0,1:T(8,128)} %param.21) | copy-start | bytes 12292
  85.4 4.7 %copy-start.7 = (s32[128,8]{0,1:T(8,128)S(1)}, s32[128,8]{0,1:T(8,128)}, u32[]{:S(2)}) copy-start(s32[128,8]{0,1:T(8,128)} %param.20) | copy-start | bytes 12292
  86.7 9.9 %all-to-all-start = ((bf16[4,128,128]{1,2,0:T(8,128)(2,1)}), bf16[4,128,128]{1,2,0:T(8,128)(2,1)S(1)}, u32[]{:S(2)}, u32[]{:S(2)}) async-start(bf16[4,128,128]{1,2,0:T(8,128)(2,1)} %copy.33), calls=%async_computation | async-start | bytes 262144 | tf_op jit(solution)/shard_map/all_to_all | solution.py:498
  98.8 1.1 copy-start.1
  153.5 9.9 %copy-start.8 = (bf16[16,128,2048]{2,1,0:T(8,128)(2,1)S(1)}, bf16[16,128,2048]{2,1,0:T(8,128)(2,1)}, u32[]{:S(2)}) copy-start(bf16[16,128,2048]{2,1,0:T(8,128)(2,1)} %get-tuple-element.65) | copy-start | bytes 25165828
  153.5 9.9 %copy-start.9 = (bf16[1,2048,768]{2,1,0:T(8,128)(2,1)S(1)}, bf16[1,2048,768]{2,1,0:T(8,128)(2,1)}, u32[]{:S(2)}) copy-start(bf16[1,2048,768]{2,1,0:T(8,128)(2,1)} %param.18) | copy-start | bytes 9437188
where the time goes:
time: 239 us; the launch traced here: 238 us
  Pallas kernels  173 us (72%)
  matrix products  31.7 us (13%)
  local copies, waits for them, and re-layouts  9.18 us (4%)
  starting transfers between devices  6.32 us (3%)
  other arithmetic  6.29 us (3%)
  waiting for transfers between devices  5.89 us (2%)
  blocking collectives  5.61 us (2%)
    pallas_call x2, Pallas kernels, gather_blocks(): pl.pallas_call(functools.partial(gather_kernel, count, kinds), out_shape=...  111 us
    pallas_call x1, Pallas kernels, scatter_sums(): pl.pallas_call(functools.partial(scatter_kernel, count), out_shape=jax.Sh...  61.9 us
    dot_general x1, matrix products, dense_experts(): gate_act = jnp.dot(rows, w_gate[e], preferred_element_type=jnp.float32)  9.84 us
    dot_general x1, matrix products, dense_experts(): up_act = jnp.dot(rows, w_up[e], preferred_element_type=jnp.float32)  8.54 us
    all_to_all x1, waiting for transfers between devices, on_device(): lax.all_to_all(heads_out, 'heads', split_axis=0, concat_axis=1, tiled=True)  5.89 us
    all_gather x1, blocking collectives, entering(): gathered = lax.all_gather(x.astype(jnp.bfloat16), axis)  5.61 us
    unnamed x25, local copies, waits for them, and re-layouts  5.56 us
  transfers between devices with their start and end apart: 2, of which 1 were waited for; matrix products, arithmetic and copies ran while one was open for 3% of the time, Pallas kernels for 0%

commit v1 on v0

--- a/solution.py
+++ b/solution.py
@@ -37,7 +37,8 @@
 VMEM_BYTES = 60 * 1024 * 1024
 ADD_ROWS = 16
 DOT_COLUMNS = 512
-LAG = 2
+HID_COLUMNS = 256
+NEAR_EIGHTHS = 5
 
 
 def place(count):
@@ -190,14 +191,109 @@
         left(zz, across, 3, {"ctx": beside})
 
 
-def scatter_kernel(
-    count, hid_ref, down_ref, weight_ref, out_ref, part_ref, from_beside, from_across, below, above, to_across, to_line,
-    beside_send, beside_recv, across_send, across_recv, line_send, below_recv, above_recv,
+def expert_kernel(
+    count, near_rows, hidden_ref, own_ref, table_ref, gate_hbm, up_hbm, down_hbm, out_ref,
+    rows_ref, part_ref, hid_ref, scale_ref, gate_ref, up_ref, down_ref,
+    from_beside, to_across, from_across, line_out, line_in, last_out, last_in,
+    local_sem, row_send, row_recv, beside_send, beside_recv, across_send, across_recv,
+    line_send, line_recv, last_send, last_recv,
 ):
     z, c, beside, across, diagonal = place(count)
+    row_count, width = own_ref.shape
+    far_rows = row_count - near_rows
+    spans = [(0, near_rows), (near_rows, far_rows)]
+    expert = c * count + z
+    local = [
+        pltpu.make_async_copy(source, target, local_sem.at[index])
+        for index, (source, target) in enumerate(
+            [
+                (gate_hbm, gate_ref),
+                (up_hbm, up_ref),
+                (down_hbm, down_ref),
+                (own_ref, rows_ref.at[z, pl.ds(pl.multiple_of(c * row_count, row_count), row_count), :]),
+            ]
+        )
+    ]
+    for copy in local:
+        copy.start()
     greet(z, count, beside, across)
 
-    def nth(index):
+    def window(cc, span):
+        first, size = spans[span]
+        return pl.ds(pl.multiple_of(cc * row_count + first, 16), size)
+
+    def row_copy(zz, cc, span, way, target, own=False):
+        first, size = spans[span]
+        slot = zz * 4 + cc
+        block = rows_ref.at[zz, window(cc, span), :]
+        return pltpu.make_async_remote_copy(
+            src_ref=own_ref.at[pl.ds(first, size), :] if own else block,
+            dst_ref=block,
+            send_sem=row_send.at[way, span, slot],
+            recv_sem=row_recv.at[span, slot],
+            device_id=target,
+            device_id_type=MESH,
+        )
+
+    def started(copy):
+        copy.start()
+
+    def left(copy):
+        copy.wait_send()
+
+    def received(zz, cc, span):
+        row_copy(zz, cc, span, 0, {"ctx": beside}).wait_recv()
+
+    def along(act, zz, cc, span, own=False):
+        @pl.when(jnp.logical_and(zz >= z, z > 0))
+        def _():
+            act(row_copy(zz, cc, span, 0, {"heads": z - 1}, own))
+
+        @pl.when(jnp.logical_and(zz <= z, z < count - 1))
+        def _():
+            act(row_copy(zz, cc, span, 1, {"heads": z + 1}, own))
+
+    def over(act, zz, cc, span, own=False):
+        act(row_copy(zz, cc, span, 2, {"ctx": across}, own))
+
+    def aside(act, zz, cc, span, own=False):
+        act(row_copy(zz, cc, span, 3, {"ctx": beside}, own))
+
+    def own_sends(act, own):
+        for span in (0, 1):
+            along(act, z, c, span, own)
+            over(act, z, c, span, own)
+        for span in (0, 1):
+            aside(act, z, c, span, own)
+
+    def own_plane_sends(act, wait):
+        for span in (1, 0):
+            if wait:
+                received(z, across, span)
+            if span == 1:
+                along(act, z, across, span)
+            aside(act, z, across, span)
+
+    def line_sends(act, wait, zz):
+        for span in (0, 1):
+            if wait:
+                received(zz, c, span)
+            along(act, zz, c, span)
+            if span == 0:
+                over(act, zz, c, span)
+            aside(act, zz, c, span)
+        if wait:
+            received(zz, across, 1)
+        along(act, zz, across, 1)
+        aside(act, zz, across, 1)
+
+    def side_sends(act, wait, zz):
+        if wait:
+            received(zz, across, 0)
+        aside(act, zz, across, 0)
+
+    def near(index):
+        index = count - 1 - index
         more = jnp.maximum(z, count - 1 - z)
         fewer = count - 1 - more
         alone = more - fewer
@@ -207,23 +303,39 @@
         offset = jnp.where(index < alone, up, both)
         return z + jnp.where(index < count - 1, offset, 0)
 
-    def compute(slot):
-        weight = weight_ref[slot][:, :1]
-
-        def tile(index, _):
+    def compute(zz):
+        for cc in range(4):
+            row = table_ref[cc * count + zz, pl.ds(expert, 1), :]
+            scale_ref[cc * row_count : (cc + 1) * row_count, :] = jnp.broadcast_to(
+                row, (HDIM, row_count)
+            ).T
+
+        inner = gate_ref.shape[1]
+
+        def hidden_tile(index, _):
+            columns = pl.ds(pl.multiple_of(index * HID_COLUMNS, HID_COLUMNS), HID_COLUMNS)
+            gate = jnp.dot(rows_ref[zz], gate_ref[:, columns], preferred_element_type=jnp.float32)
+            up = jnp.dot(rows_ref[zz], up_ref[:, columns], preferred_element_type=jnp.float32)
+            scale = jnp.concatenate([scale_ref[...]] * (HID_COLUMNS // HDIM), axis=1)
+            hid_ref[:, columns] = (jax.nn.silu(gate) * up * scale).astype(hid_ref.dtype)
+            return 0
+
+        lax.fori_loop(0, inner // HID_COLUMNS, hidden_tile, 0)
+
+        def out_tile(index, _):
             columns = pl.ds(pl.multiple_of(index * DOT_COLUMNS, DOT_COLUMNS), DOT_COLUMNS)
             product = jnp.dot(
-                hid_ref[slot], down_ref[:, columns], preferred_element_type=jnp.float32
+                hid_ref[...], down_ref[:, columns], preferred_element_type=jnp.float32
             )
-            part_ref[slot, :, columns] = (weight * product).astype(part_ref.dtype)
+            part_ref[zz, :, columns] = product.astype(part_ref.dtype)
             return 0
 
-        lax.fori_loop(0, down_ref.shape[1] // DOT_COLUMNS, tile, 0)
+        lax.fori_loop(0, width // DOT_COLUMNS, out_tile, 0)
 
     def beside_copy(kind, zz):
         cc = diagonal if kind == 0 else beside
         return pltpu.make_async_remote_copy(
-            src_ref=part_ref.at[cc * count + zz],
+            src_ref=part_ref.at[zz, pl.ds(pl.multiple_of(cc * row_count, row_count), row_count), :],
             dst_ref=from_beside.at[kind, zz],
             send_sem=beside_send.at[kind, zz],
             recv_sem=beside_recv.at[kind, zz],
@@ -241,23 +353,26 @@
             device_id_type=MESH,
         )
 
-    def up_copy(zz):
+    line_spans = [(0, near_rows), (near_rows, far_rows), (row_count, far_rows)]
+
+    def line_copy(side, zz, chunk):
+        first, size = line_spans[chunk]
         return pltpu.make_async_remote_copy(
-            src_ref=to_line.at[zz],
-            dst_ref=below.at[zz],
-            send_sem=line_send.at[zz],
-            recv_sem=below_recv.at[zz],
-            device_id={"heads": z + 1},
+            src_ref=line_out.at[zz, pl.ds(first, size), :],
+            dst_ref=line_in.at[side, zz, pl.ds(first, size), :],
+            send_sem=line_send.at[chunk, zz],
+            recv_sem=line_recv.at[chunk, side, zz],
+            device_id={"heads": z + 1 - 2 * side},
             device_id_type=MESH,
         )
 
-    def down_copy(zz):
+    def last_copy():
         return pltpu.make_async_remote_copy(
-            src_ref=to_line.at[zz],
-            dst_ref=above.at[zz],
-            send_sem=line_send.at[zz],
-            recv_sem=above_recv.at[zz],
-            device_id={"heads": z - 1},
+            src_ref=last_out,
+            dst_ref=last_in,
+            send_sem=last_send,
+            recv_sem=last_recv,
+            device_id={"ctx": across},
             device_id_type=MESH,
         )
 
@@ -272,81 +387,164 @@
 
         lax.fori_loop(0, target.shape[0] // ADD_ROWS, chunk, 0)
 
-    def project(zz):
-        compute(diagonal * count + zz)
+    def chip_sources(zz, chunk):
+        cc, kind = (across, 0) if chunk == 2 else (c, 1)
+        span = 0 if chunk == 0 else 1
+        first, size = spans[span]
+        sources = [
+            part_ref.at[zz, window(cc, span), :],
+            from_beside.at[kind, zz, pl.ds(first, size), :],
+        ]
+        return sources + ([from_across.at[zz]] if chunk == 0 else [])
+
+    def exchange(zz):
         beside_copy(0, zz).start()
-        compute(across * count + zz)
+        beside_copy(1, zz).start()
         beside_copy(0, zz).wait_recv()
-        add(to_across.at[zz], [part_ref.at[across * count + zz], from_beside.at[0, zz]])
+        add(
+            to_across.at[zz],
+            [part_ref.at[zz, window(across, 0), :], from_beside.at[0, zz, pl.ds(0, near_rows), :]],
+        )
         across_copy(zz).start()
-        compute(beside * count + zz)
-        beside_copy(1, zz).start()
-        compute(c * count + zz)
-
-    def onward(zz, copy, arriving, first, sources):
-        @pl.when(first)
-        def _():
-            add(to_line.at[zz], sources)
-
-        @pl.when(jnp.logical_not(first))
-        def _():
-            copy(zz).wait_recv()
-            add(to_line.at[zz], sources + [arriving.at[zz]])
-
-        copy(zz).start()
-
-    def pass_line(zz):
         beside_copy(1, zz).wait_recv()
-        across_copy(zz).wait_recv()
-        sources = [part_ref.at[c * count + zz], from_beside.at[1, zz], from_across.at[zz]]
-
-        @pl.when(zz > z)
-        def _():
-            onward(zz, up_copy, below, z == 0, sources)
-
-        @pl.when(zz < z)
-        def _():
-            onward(zz, down_copy, above, z == count - 1, sources)
-
-        @pl.when(zz == z)
-        def _():
-            add(out_ref, sources)
-
-            @pl.when(z > 0)
+
+    def line_block(side, zz, chunk):
+        first, size = line_spans[chunk]
+        return line_in.at[side, zz, pl.ds(first, size), :]
+
+    def starts(side):
+        return z == side * (count - 1)
+
+    def pass_line(side, zz):
+        for chunk in (1, 2, 0):
+            if chunk == 0:
+                across_copy(zz).wait_recv()
+
+            @pl.when(jnp.logical_not(starts(side)))
             def _():
-                up_copy(zz).wait_recv()
-                add(out_ref, [out_ref, below.at[zz]])
-
-            @pl.when(z < count - 1)
+                line_copy(side, zz, chunk).wait_recv()
+
+            first, size = line_spans[chunk]
+            add(
+                line_out.at[zz, pl.ds(first, size), :],
+                chip_sources(zz, chunk) + [line_block(side, zz, chunk)],
+            )
+            line_copy(side, zz, chunk).start()
+
+    own_sends(started, True)
+
+    for side in (0, 1):
+
+        @pl.when(starts(side))
+        def _():
+            def clear(index, _):
+                line_in[side, index] = jnp.zeros(line_in.shape[2:], line_in.dtype)
+                return 0
+
+            lax.fori_loop(0, count, clear, 0)
+
+    for copy in local:
+        copy.wait()
+    own_plane_sends(started, True)
+
+    def distance(zz):
+        return jnp.abs(zz - z)
+
+    end_side = jnp.where(z == 0, 0, 1)
+    at_end = jnp.logical_or(z == 0, z == count - 1)
+
+    def step(index, _):
+        zz = near(index)
+        before = near(jnp.maximum(index - 1, 0))
+        after = near(jnp.minimum(index + 1, count - 1))
+        opens = jnp.logical_and(index > 0, distance(zz) != distance(before))
+
+        @pl.when(opens)
+        def _():
+            line_sends(started, True, zz)
+
+        @pl.when(jnp.logical_and(opens, jnp.logical_and(index < count - 1, distance(after) == distance(zz))))
+        def _():
+            line_sends(started, True, after)
+
+        @pl.when(jnp.logical_and(at_end, index > 1))
+        def _():
+            pass_line(end_side, before)
+
+        @pl.when(index > 0)
+        def _():
+            side_sends(started, True, zz)
+
+        for span in (0, 1):
+            received(zz, beside, span)
+            received(zz, diagonal, span)
+        compute(zz)
+        exchange(zz)
+        return 0
+
+    lax.fori_loop(0, count, step, 0)
+
+    def link(index, _):
+        key = index // 2 + 1
+        low = z < count - 1 - z
+        side = jnp.where(low, index % 2, 1 - index % 2)
+        zz = jnp.where(side == 0, key, count - 1 - key)
+        valid = jnp.where(side == 0, zz > z, zz < z)
+        done = jnp.logical_and(starts(side), key < count - 1)
+
+        @pl.when(jnp.logical_and(valid, jnp.logical_not(done)))
+        def _():
+            pass_line(side, zz)
+
+        return 0
+
+    lax.fori_loop(0, 2 * (count - 1), link, 0)
+
+    def both_sides(chunk):
+        for side in (0, 1):
+
+            @pl.when(jnp.logical_not(starts(side)))
             def _():
-                down_copy(zz).wait_recv()
-                add(out_ref, [out_ref, above.at[zz]])
-
-    def step(index, _):
-        @pl.when(index < count)
-        def _():
-            project(nth(index))
-
-        @pl.when(index >= LAG)
-        def _():
-            pass_line(nth(index - LAG))
-
-        return 0
-
-    lax.fori_loop(0, count + LAG, step, 0)
-
-    for zz in range(count):
+                line_copy(side, z, chunk).wait_recv()
+
+        return [line_block(side, z, chunk) for side in (0, 1)]
+
+    sides = both_sides(2)
+    add(last_out, chip_sources(z, 2) + sides)
+    last_copy().start()
+    across_copy(z).wait_recv()
+    sides = both_sides(0)
+    add(
+        out_ref.at[pl.ds(0, near_rows), :],
+        [hidden_ref.at[pl.ds(0, near_rows), :]] + chip_sources(z, 0) + sides,
+    )
+    sides = both_sides(1)
+    last_copy().wait_recv()
+    add(
+        out_ref.at[pl.ds(near_rows, far_rows), :],
+        [hidden_ref.at[pl.ds(near_rows, far_rows), :]] + chip_sources(z, 1) + sides + [last_in],
+    )
+
+    last_copy().wait_send()
+    own_sends(left, True)
+    own_plane_sends(left, False)
+
+    def drain(zz, _):
         beside_copy(0, zz).wait_send()
         beside_copy(1, zz).wait_send()
         across_copy(zz).wait_send()
 
-        @pl.when(zz > z)
-        def _():
-            up_copy(zz).wait_send()
-
-        @pl.when(zz < z)
-        def _():
-            down_copy(zz).wait_send()
+        @pl.when(zz != z)
+        def _():
+            line_sends(left, False, zz)
+            side_sends(left, False, zz)
+            side = jnp.where(zz > z, 0, 1)
+            for chunk in range(3):
+                line_copy(side, zz, chunk).wait_send()
+
+        return 0
+
+    lax.fori_loop(0, count, drain, 0)
 
 
 def gather_blocks(kinds, operands, collective_id, name):
@@ -374,61 +572,68 @@
     )(*operands)
 
 
-def scatter_sums(hid, down, weights):
+def near_share(row_count):
+    return max(16, row_count * NEAR_EIGHTHS // 8 // 16 * 16)
+
+
+def run_experts(hidden, normed, tables, w_gate, w_up, w_down):
     count = lax.axis_size("heads")
-    devices, rows, _ = hid.shape
-    block = (rows, down.shape[1])
+    row_count, width = normed.shape
+    inner = w_gate.shape[1]
+    near_rows = near_share(row_count)
+    far_rows = row_count - near_rows
     dma = pltpu.SemaphoreType.DMA
+    kind = normed.dtype
+    vmem, anywhere = pl.BlockSpec(memory_space=pltpu.VMEM), pl.BlockSpec(memory_space=pl.ANY)
     return pl.pallas_call(
-        functools.partial(scatter_kernel, count),
-        out_shape=jax.ShapeDtypeStruct(block, jnp.float32),
-        in_specs=[pl.BlockSpec(memory_space=pltpu.VMEM)] * 3,
-        out_specs=pl.BlockSpec(memory_space=pltpu.VMEM),
+        functools.partial(expert_kernel, count, near_rows),
+        out_shape=jax.ShapeDtypeStruct((row_count, width), kind),
+        in_specs=[vmem] * 3 + [anywhere] * 3,
+        out_specs=vmem,
         scratch_shapes=[
-            pltpu.VMEM((devices,) + block, hid.dtype),
-            pltpu.VMEM((2, count) + block, hid.dtype),
-        ]
-        + [pltpu.VMEM((count,) + block, hid.dtype)] * 5
-        + [dma((2, count))] * 2
-        + [dma((count,))] * 5,
+            pltpu.VMEM((count, 4 * row_count, width), kind),
+            pltpu.VMEM((count, 4 * row_count, width), kind),
+            pltpu.VMEM((4 * row_count, inner), kind),
+            pltpu.VMEM((4 * row_count, HDIM), jnp.float32),
+            pltpu.VMEM(w_gate.shape, kind),
+            pltpu.VMEM(w_up.shape, kind),
+            pltpu.VMEM(w_down.shape, kind),
+            pltpu.VMEM((2, count, row_count, width), kind),
+            pltpu.VMEM((count, near_rows, width), kind),
+            pltpu.VMEM((count, near_rows, width), kind),
+            pltpu.VMEM((count, row_count + far_rows, width), kind),
+            pltpu.VMEM((2, count, row_count + far_rows, width), kind),
+            pltpu.VMEM((far_rows, width), kind),
+            pltpu.VMEM((far_rows, width), kind),
+            dma((4,)),
+            dma((4, 2, 4 * count)),
+            dma((2, 4 * count)),
+            dma((2, count)),
+            dma((2, count)),
+            dma((count,)),
+            dma((count,)),
+            dma((3, count)),
+            dma((3, 2, count)),
+            dma(()),
+            dma(()),
+        ],
         compiler_params=pltpu.CompilerParams(
-            collective_id=1, has_side_effects=True, vmem_limit_bytes=VMEM_BYTES
+            collective_id=0, has_side_effects=True, vmem_limit_bytes=VMEM_BYTES
         ),
-        name="scatter_sums",
-    )(hid, down, weights)
-
-
-def gather_inputs(tokens, w_out):
-    if lax.axis_size("ctx") == 4 and w_out.shape[0] % 64 == 0:
-        slab, w_rows = gather_blocks(("line", "share"), (tokens, w_out), 2, "gather_inputs")
-        width = tokens.shape[1]
-        return slab.reshape(-1, width), w_rows.reshape(-1, w_out.shape[1])
-    return [lax.all_gather(value, "heads", axis=0, tiled=True) for value in (tokens, w_out)]
-
-
-def dense_experts(
-    hidden_float, normed, w_gate, w_up, w_down, expert_ids, gate_weights, expert_count
-):
-    axes = ("ctx", "heads")
-    exp_local = w_gate.shape[0]
+        name="run_experts",
+    )(hidden, normed, tables, w_gate, w_up, w_down)
+
+
+def expert_table(expert_ids, gate_weights, expert_count):
     chosen = expert_ids[:, :, None] == jnp.arange(expert_count, dtype=jnp.int32)
-    table = jnp.sum(jnp.where(chosen, gate_weights[:, :, None], 0.0), axis=1)
-    first = lax.axis_index(axes) * exp_local
-    rows, tables = gather_blocks(
-        ("group", "group"), (normed, table.T), 0, "gather_rows"
-    )
-    device_count, row_count, width = rows.shape
-    rows = rows.reshape(device_count * row_count, width)
-    routed = 0.0
-    for e in range(exp_local):
-        gate_act = jnp.dot(rows, w_gate[e], preferred_element_type=jnp.float32)
-        up_act = jnp.dot(rows, w_up[e], preferred_element_type=jnp.float32)
-        hid = (jax.nn.silu(gate_act) * up_act).astype(jnp.bfloat16)
-        weight = lax.dynamic_index_in_dim(tables, first + e, 1, False)
-        weight = jnp.broadcast_to(weight[:, :, None], (device_count, row_count, HDIM))
-        hid = hid.reshape(device_count, row_count, hid.shape[1])
-        routed = routed + scatter_sums(hid, w_down[e], weight)
-    return (hidden_float + routed).astype(jnp.bfloat16)
+    return jnp.sum(jnp.where(chosen, gate_weights[:, :, None], 0.0), axis=1).T
+
+
+def gather_inputs(tokens, w_out, table):
+    slab, w_rows, tables = gather_blocks(
+        ("line", "share", "group"), (tokens, w_out, table), 2, "gather_inputs"
+    )
+    return slab.reshape(-1, tokens.shape[1]), w_rows.reshape(-1, w_out.shape[1]), tables
 
 
 def on_device(
@@ -438,7 +643,28 @@
     inner_width = w_qkv.shape[2]
     local_heads = inner_width // HDIM
     w_flat = w_qkv.reshape(model_width, 3 * inner_width)
-    slab, w_rows = gather_inputs(tokens, w_out)
+    ctx_count = lax.axis_size("ctx")
+    head_count = lax.axis_size("heads")
+    exp_local = w_gate.shape[0]
+    devices = ctx_count * head_count
+    expert_count = exp_local * devices
+    top_count = expert_ids.shape[1]
+    capacity = max(2, 2 * row_count * top_count // expert_count)
+    dense = (
+        ctx_count == 4
+        and exp_local == 1
+        and row_count % HDIM == 0
+        and w_out.shape[0] % 64 == 0
+        and w_gate.shape[2] % HID_COLUMNS == 0
+        and row_count * devices <= expert_count * capacity
+    )
+    if dense:
+        table = expert_table(expert_ids, gate_weights, expert_count)
+        slab, w_rows, tables = gather_inputs(tokens, w_out, table)
+    else:
+        slab, w_rows = [
+            lax.all_gather(value, "heads", axis=0, tiled=True) for value in (tokens, w_out)
+        ]
     projected = jnp.dot(
         slab,
         w_flat,
@@ -504,17 +730,8 @@
     hidden_state = (tokens.astype(jnp.float32) + attn).astype(jnp.bfloat16)
     hidden_float = hidden_state.astype(jnp.float32)
     normed = normalize(hidden_float).astype(jnp.bfloat16)
-    ctx_count = lax.axis_size("ctx")
-    head_count = lax.axis_size("heads")
-    exp_local = w_gate.shape[0]
-    expert_count = exp_local * ctx_count * head_count
-    top_count = expert_ids.shape[1]
-    capacity = max(2, 2 * row_count * top_count // expert_count)
-    devices = ctx_count * head_count
-    if ctx_count == 4 and row_count * devices <= expert_count * capacity:
-        return dense_experts(
-            hidden_float, normed, w_gate, w_up, w_down, expert_ids, gate_weights, expert_count
-        )
+    if dense:
+        return run_experts(hidden_state, normed, tables, w_gate[0], w_up[0], w_down[0])
     picks = expert_ids.reshape(-1)
     onehot = (picks[:, None] == jnp.arange(expert_count, dtype=jnp.int32)[None, :]).astype(
         jnp.int32

time: 239 us -> 223 us (0.933)
  matrix products: 31.7 us -> 5.39 us
  Pallas kernels: 173 us -> 193 us
  blocking collectives: 5.61 us -> 14.5 us
  waiting for transfers between devices: 5.89 us -> 0.01 us
  local copies, waits for them, and re-layouts: 9.18 us -> 4.08 us
  other arithmetic: 6.29 us -> 2.14 us
  starting transfers between devices: 6.32 us -> 2.5 us
    pallas_call x1, Pallas kernels: 61.9 us -> 134 us  [run_experts(): pl.pallas_call(functools.partial(expert_kernel, count, near_rows), out_sh...]
    pallas_call x2 -> x1, Pallas kernels: 111 us -> 60 us  [gather_blocks(): pl.pallas_call(functools.partial(gather_kernel, count, kinds), out_shape=...]
    dot_general x2 -> x0, matrix products: 18.4 us -> none  [the longest x1 9.84 us: dense_experts(): gate_act = jnp.dot(rows, w_gate[e], preferred_element_type=jnp.float32)]
    all_to_all x0 -> x1, blocking collectives: none -> 9.05 us  [on_device(): lax.all_to_all(heads_out, 'heads', split_axis=0, concat_axis=1, tiled=True)]
    all_to_all x1 -> x0, waiting for transfers between devices: 5.89 us -> none  [on_device(): lax.all_to_all(heads_out, 'heads', split_axis=0, concat_axis=1, tiled=True)]
    all_to_all x1 -> x0, starting transfers between devices: 3.33 us -> none  [on_device(): lax.all_to_all(heads_out, 'heads', split_axis=0, concat_axis=1, tiled=True)]
    convert_element_type x1 -> x0, other arithmetic: 2.45 us -> none  [dense_experts(): return (hidden_float + routed).astype(jnp.bfloat16)]
    unnamed x25 -> x18, local copies, waits for them, and re-layouts: 5.56 us -> 3.9 us
  transfers between devices with their start and end apart: 2 -> 1, of which waited for: 1 -> 0; matrix products, arithmetic and copies ran while one was open for 3% -> 0% of each run, Pallas kernels for 0% -> 0%
where the time goes in v1:
time: 223 us; the launch traced here: 222 us
  Pallas kernels  193 us (87%)
  blocking collectives  14.5 us (7%)
  matrix products  5.39 us (2%)
  local copies, waits for them, and re-layouts  4.08 us (2%)
  starting transfers between devices  2.5 us (1%)
    pallas_call x1, Pallas kernels, run_experts(): pl.pallas_call(functools.partial(expert_kernel, count, near_rows), out_sh...  134 us
    pallas_call x1, Pallas kernels, gather_blocks(): pl.pallas_call(functools.partial(gather_kernel, count, kinds), out_shape=...  60 us
    all_to_all x1, blocking collectives, on_device(): lax.all_to_all(heads_out, 'heads', split_axis=0, concat_axis=1, tiled=True)  9.05 us
    all_gather x1, blocking collectives, entering(): gathered = lax.all_gather(x.astype(jnp.bfloat16), axis)  5.42 us
  transfers between devices with their start and end apart: 1, of which 0 were waited for; matrix products, arithmetic and copies ran while one was open for 0% of the time, Pallas kernels for 0%

profile of v1, /device:TPU:0, one launch (start us, length us, event | category | flops | bytes accessed | tf_op | source)
XLA Modules:
  0.0 222.3 jit_solution(9118038495062521677)
XLA Ops:
  0.0 1.7 copy.27
  1.8 0.6 select_reduce_fusion
  2.4 60.0 %gather_inputs.1 = (bf16[4,128,2048]{2,1,0:T(8,128)(2,1)}, bf16[16,32,2048]{2,1,0:T(8,128)(2,1)}, f32[16,16,128]{2,1,0:T(8,128)}) custom-call(bf16[128,2048]{1,0:T(8,128)(2,1)} %refs_0_.1, bf16[128,2048]{1,0:T(8,128)(2,1)} %refs_1_.1, f32[16,128]{1,0:T(8,128)} %bitcast.95), custom_call_target="tpu_custom_call" | custom-call | tf_op jit(solution)/shard_map/gather_inputs/pallas_call | solution.py:557
  62.4 2.6 %convolution_convert_fusion = bf16[512,384]{0,1:T(8,128)(2,1)S(1)} fusion(bf16[512,2048]{1,0:T(8,128)(2,1)} %bitcast.96, bf16[2048,384]{0,1:T(8,128)(2,1)S(1)} %bitcast.81), kind=kOutput, calls=%fused_computation.15 | convolution fusion | flops 805502976 | bytes 4063232 | tf_op jit(solution)/shard_map/dot_general | solution.py:668
  65.0 0.0 copy-start.4
  65.0 0.1 copy.34
  65.1 0.1 copy.35
  65.3 0.0 copy-start.3
  65.3 2.5 %collective-permute-start = (bf16[2,1,512,128]{3,2,1,0:T(8,128)(2,1)S(1)}, bf16[2,1,512,128]{3,2,1,0:T(8,128)(2,1)S(1)}, u32[]{:S(2)}, u32[]{:S(2)}) collective-permute-start(bf16[2,1,512,128]{3,2,1,0:T(8,128)(2,1)S(1)} %pad_maximum_fusion), channel_id=1, source_target_pairs={{0,4},{4,8},{8,12},{1,5},{5,9},{9,13},{2,6},{6,10},{10,14},{3,7},{... | collective-permute-start | bytes 786440 | tf_op jit(solution)/shard_map/ppermute | solution.py:29
  67.8 0.2 convolution_convert_fusion.1
  68.0 5.4 %all-gather = bf16[512,128]{1,0:T(8,128)(2,1)S(1)} all-gather(bf16[128,128]{1,0:T(8,128)(2,1)S(1)} %convolution_convert_fusion.1), channel_id=2, replica_groups=mesh['groups'=2,'ctx'=4,'heads'=4] {'ctx'}, dimensions={0}, use_global_device_ids=true | all-gather | bytes 163840 | tf_op jit(solution)/shard_map/all_gather | solution.py:17
  73.5 0.3 fusion.21
  73.8 0.5 multiply_reduce_fusion
  74.4 0.6 fusion.33
  75.0 0.5 fusion.4
  75.5 0.0 copy-start.2
  75.6 0.6 fusion.8
  76.1 0.1 copy.33
  76.3 9.0 %all_to_all.19 = bf16[4,128,128]{1,2,0:T(8,128)(2,1)S(1)} all-to-all(bf16[4,128,128]{1,2,0:T(8,128)(2,1)S(1)} %copy.33), channel_id=1, replica_groups=mesh['groups'=2,'ctx'=4,'heads'=4] {'heads'}, dimensions={0} | all-to-all | bytes 262144 | tf_op jit(solution)/shard_map/all_to_all | solution.py:724
  85.3 0.6 fusion.9
  85.9 0.0 copy-start
  85.9 0.9 fusion.10.own_ref
  86.9 133.5 %run_experts.1 = bf16[128,2048]{1,0:T(8,128)(2,1)} custom-call(bf16[128,2048]{1,0:T(8,128)(2,1)} %copy-done, bf16[128,2048]{1,0:T(8,128)(2,1)} %fusion.10.own_ref, f32[16,16,128]{2,1,0:T(8,128)} %get-tuple-element.64.table_ref, bf16[2048,768]{1,0:T(8,128)(2,1)} %bitcast.77, bf16[2048,768]{1,0:T(8,128)(2,1)} %bitcast.78, bf16[768,2048]{1,0:T(8,128)(2,1)} %bitcast.79), custom_call_target="tpu_custom_call" | custom-call | tf_op jit(solution)/shard_map/run_experts/pallas_call | solution.py:588
  220.4 1.9 copy.43
  (20 shorter events, 0.1 us)
Async XLA Ops:
  0.0 1.8 copy-start.6
  0.0 1.8 copy-start.5
  65.0 8.5 %copy-start.4 = (f32[1,128,128]{2,1,0:T(8,128)S(1)}, f32[1,128,128]{2,1,0:T(8,128)}, u32[]{:S(2)}) copy-start(f32[1,128,128]{2,1,0:T(8,128)} %param.13) | copy-start | bytes 196612
  65.3 9.1 %copy-start.3 = (bf16[2,512,128]{2,1,0:T(8,128)(2,1)S(1)}, bf16[2,512,128]{2,1,0:T(8,128)(2,1)}, u32[]{:S(2)}) copy-start(bf16[2,512,128]{2,1,0:T(8,128)(2,1)} %param.14) | copy-start | bytes 786436
  65.3 9.0 %collective-permute-start = (bf16[2,1,512,128]{3,2,1,0:T(8,128)(2,1)S(1)}, bf16[2,1,512,128]{3,2,1,0:T(8,128)(2,1)S(1)}, u32[]{:S(2)}, u32[]{:S(2)}) collective-permute-start(bf16[2,1,512,128]{3,2,1,0:T(8,128)(2,1)S(1)} %pad_maximum_fusion), channel_id=1, source_target_pairs={{0,4},{4,8},{8,12},{1,5},{5,9},{9,13},{2,6},{6,10},{10,14},{3,7},{... | collective-permute-start | bytes 786440 | tf_op jit(solution)/shard_map/ppermute | solution.py:29
  75.5 9.8 %copy-start.1 = (bf16[16,32,2048]{2,1,0:T(8,128)(2,1)S(1)}, bf16[16,32,2048]{2,1,0:T(8,128)(2,1)}, u32[]{:S(2)}) copy-start(bf16[16,32,2048]{2,1,0:T(8,128)(2,1)} %get-tuple-element.63) | copy-start | bytes 6291460
  75.5 9.8 %copy-start.2 = (bf16[128,2048]{1,0:T(8,128)(2,1)S(1)}, bf16[128,2048]{1,0:T(8,128)(2,1)}, u32[]{:S(2)}) copy-start(bf16[128,2048]{1,0:T(8,128)(2,1)} %refs_0_.1) | copy-start | bytes 1572868
  85.9 1.0 copy-start

commit v2 on v1

--- a/solution.py
+++ b/solution.py
@@ -35,9 +35,13 @@
 
 MESH = pl.DeviceIdType.MESH
 VMEM_BYTES = 60 * 1024 * 1024
+FRONT_BYTES = 60 * 1024 * 1024
 ADD_ROWS = 16
 DOT_COLUMNS = 512
 HID_COLUMNS = 256
+LOAD_TIME = 0.6
+UNIT_TIME = 0.75
+SLACK = 0.05
 NEAR_EIGHTHS = 5
 
 
@@ -70,125 +74,422 @@
     pl.semaphore_wait(barrier, 2 + jnp.minimum(z, 1) + jnp.minimum(count - 1 - z, 1))
 
 
-def gather_kernel(count, kinds, *refs):
-    size = len(kinds)
-    groups = [refs[first * size : (first + 1) * size] for first in range(4)]
-    own_sem = refs[4 * size]
+def nearest(count, z, index):
+    index = count - 1 - index
+    more = jnp.maximum(z, count - 1 - z)
+    fewer = count - 1 - more
+    alone = more - fewer
+    paired = jnp.maximum(index - alone, 0)
+    up = jnp.where(z + more < count, more - index, index - more)
+    both = (fewer - paired // 2) * (1 - 2 * (paired % 2))
+    offset = jnp.where(index < alone, up, both)
+    return z + jnp.where(index < count - 1, offset, 0)
+
+
+def attend_kernel(
+    count, tokens_ref, share_hbm, table_ref, state_ref, past_hbm, qkv_hbm,
+    hidden_ref, normed_ref, tables_ref,
+    slab_ref, qkv_ref, w_ref, query_ref, kv_ref, before_ref, inside_ref, linear_ref,
+    state_out, states_in, heads_out, heads_in,
+    local_sem, token_send, token_recv, share_send, share_recv,
+    tail_send, tail_recv, state_send, state_recv, head_send, head_recv,
+):
     z, c, beside, across, diagonal = place(count)
-    greet(z, count, beside, across)
-
-    def origin(kind, source, full):
-        if kind != "share":
-            return source
-        share = full.shape[1]
-        return source.at[pl.ds(pl.multiple_of(c * share, share), share), :]
-
-    def slot_of(kind, zz, cc):
-        return {"group": cc * count + zz, "share": zz * 4 + cc, "line": zz}[kind]
-
-    def copies(zz, cc, way, target, own=False):
-        result = []
-        for kind, source, full, send, recv in zip(kinds, *groups):
-            if kind == "line" and (way > 1 or cc is not c):
-                continue
-            slot = slot_of(kind, zz, cc)
-            result.append(
-                pltpu.make_async_remote_copy(
-                    src_ref=origin(kind, source, full) if own else full.at[slot],
-                    dst_ref=full.at[slot],
-                    send_sem=send.at[way, slot],
-                    recv_sem=recv.at[slot],
-                    device_id=target,
-                    device_id_type=MESH,
-                )
-            )
-        return result
-
-    def start(zz, cc, way, target, own=False):
-        for copy in copies(zz, cc, way, target, own):
-            copy.start()
-
-    def arrived(zz, cc):
-        for copy in copies(zz, cc, 0, {"ctx": beside}):
-            copy.wait_recv()
-
-    def left(zz, cc, way, target):
-        for copy in copies(zz, cc, way, target):
-            copy.wait_send()
-
-    def along(act, down, up, zz, **options):
-        if down:
-
-            @pl.when(z > 0)
-            def _():
-                act(zz, c, 0, {"heads": z - 1}, **options)
-
-        if up:
-
-            @pl.when(z < count - 1)
-            def _():
-                act(zz, c, 1, {"heads": z + 1}, **options)
-
-        act(zz, c, 2, {"ctx": across}, **options)
-        act(zz, c, 3, {"ctx": beside}, **options)
+    row_count, width = tokens_ref.shape
+    slab_rows = count * row_count
+    share = w_ref.shape[0] // (4 * count)
+
+    def rows_of(index, size):
+        return pl.ds(pl.multiple_of(index * size, size), size)
+
+    def share_block(kind, zz, cc):
+        if kind == 0:
+            return w_ref.at[rows_of(zz * 4 + cc, share), :]
+        return tables_ref.at[cc * count + zz]
+
+    def share_source(kind):
+        return table_ref if kind else share_hbm.at[rows_of(c, share), :]
 
     local = [
-        pltpu.make_async_copy(
-            origin(kind, source, full), full.at[slot_of(kind, z, c)], own_sem.at[index]
-        )
-        for index, (kind, source, full) in enumerate(zip(kinds, *groups[:2]))
+        pltpu.make_async_copy(source, target, local_sem.at[index])
+        for index, (source, target) in enumerate(
+            [(qkv_hbm.at[one], qkv_ref.at[:, one * HDIM : (one + 1) * HDIM]) for one in range(3)]
+            + [(tokens_ref, slab_ref.at[z])]
+            + [(share_source(kind), share_block(kind, z, c)) for kind in (0, 1)]
+        )
     ]
+    past_copy = pltpu.make_async_copy(past_hbm, before_ref, local_sem.at[6])
     for copy in local:
         copy.start()
-    along(start, True, True, z, own=True)
-
-    def over(zz):
-        arrived(zz, across)
-        start(zz, across, 3, {"ctx": beside})
-
-    for d in range(1, count + 1):
-        if d < count:
-
-            @pl.when(z >= d)
-            def _():
-                arrived(z - d, c)
-                along(start, False, True, z - d)
-
-            @pl.when(z + d < count)
-            def _():
-                arrived(z + d, c)
-                along(start, True, False, z + d)
-
-        if d == 1:
-            over(z)
-        else:
-
-            @pl.when(z >= d - 1)
-            def _():
-                over(z - d + 1)
-
-            @pl.when(z + d - 1 < count)
-            def _():
-                over(z + d - 1)
-
+
+    @pl.when(c == 0)
+    def _():
+        past_copy.start()
+
+    barrier = pltpu.get_barrier_semaphore()
+    for target in (beside, across, diagonal):
+        pl.semaphore_signal(barrier, inc=1, device_id={"ctx": target}, device_id_type=MESH)
     for zz in range(count):
-        arrived(zz, beside)
-        arrived(zz, diagonal)
+
+        @pl.when(zz != z)
+        def _():
+            pl.semaphore_signal(barrier, inc=1, device_id={"heads": zz}, device_id_type=MESH)
+
+    pl.semaphore_wait(barrier, 3 + count - 1)
+
+    def remote(source, target, send, recv, device):
+        return pltpu.make_async_remote_copy(
+            src_ref=source, dst_ref=target, send_sem=send, recv_sem=recv,
+            device_id=device, device_id_type=MESH,
+        )
+
+    def started(copy):
+        copy.start()
+
+    def left(copy):
+        copy.wait_send()
+
+    def along(act, zz, copy):
+        @pl.when(jnp.logical_and(zz >= z, z > 0))
+        def _():
+            act(copy(0, {"heads": z - 1}))
+
+        @pl.when(jnp.logical_and(zz <= z, z < count - 1))
+        def _():
+            act(copy(1, {"heads": z + 1}))
+
+    def token_copy(zz, own=False):
+        def copy(way, device):
+            source = tokens_ref if own else slab_ref.at[zz]
+            return remote(source, slab_ref.at[zz], token_send.at[way, zz], token_recv.at[zz], device)
+
+        return copy
+
+    def share_copy(kind, zz, cc, own=False):
+        def copy(way, device):
+            block = share_block(kind, zz, cc)
+            slot = zz * 4 + cc
+            source = share_source(kind) if own else block
+            return remote(
+                source, block, share_send.at[kind, way, slot], share_recv.at[kind, slot], device
+            )
+
+        return copy
+
+    def aside(act, zz, cc, own=False):
+        for kind in (0, 1):
+            act(share_copy(kind, zz, cc, own)(3, {"ctx": beside}))
+
+    def share_relay(act, zz, own=False):
+        for kind in (0, 1):
+            act(share_copy(kind, zz, c, own)(2, {"ctx": across}))
+        aside(act, zz, c, own)
+
+    def share_along(act, zz, own=False):
+        for kind in (0, 1):
+            along(act, zz, share_copy(kind, zz, c, own))
+
+    def share_received(zz, cc):
+        for kind in (0, 1):
+            share_copy(kind, zz, cc)(3, {"ctx": beside}).wait_recv()
+
+    def at_distance(distance, act):
+        @pl.when(z >= distance)
+        def _():
+            act(z - distance)
+
+        @pl.when(z + distance < count)
+        def _():
+            act(z + distance)
+
+    def share_stage(distance):
+        def one(zz):
+            share_received(zz, c)
+            share_along(started, zz)
+            share_relay(started, zz)
+
+        at_distance(distance, one)
+
+    def share_over(zz):
+        share_received(zz, across)
+        aside(started, zz, across)
+
+    along(started, z, token_copy(z, True))
+    share_relay(started, z, True)
     for copy in local:
         copy.wait()
-    along(left, True, True, z)
-    for d in range(1, count):
-
-        @pl.when(z >= d)
+
+    def project(zz):
+        product = jnp.dot(slab_ref[zz], qkv_ref[...], preferred_element_type=jnp.float32)
+        product = product.astype(query_ref.dtype)
+        rows = rows_of(zz, row_count)
+        query_ref[rows, :] = product[:, :HDIM]
+        kv_ref[0, rows, :] = product[:, HDIM : 2 * HDIM]
+        kv_ref[1, rows, :] = product[:, 2 * HDIM :]
+
+    def token_relay(zz):
+        token_copy(zz)(0, {"heads": z - 1}).wait_recv()
+        along(started, zz, token_copy(zz))
+
+    def step(index, _):
+        zz = nearest(count, z, index)
+        last = nearest(count, z, jnp.maximum(index - 1, 0))
+        after = nearest(count, z, jnp.minimum(index + 1, count - 1))
+        opens = jnp.logical_and(index > 0, jnp.abs(zz - z) != jnp.abs(last - z))
+        double = jnp.logical_and(index < count - 1, jnp.abs(after - z) == jnp.abs(zz - z))
+
+        @pl.when(opens)
         def _():
-            along(left, False, True, z - d)
-
-        @pl.when(z + d < count)
+            token_relay(zz)
+
+        @pl.when(jnp.logical_and(opens, double))
         def _():
-            along(left, True, False, z + d)
+            token_relay(after)
+
+        project(zz)
+        return 0
+
+    lax.fori_loop(0, count, step, 0)
+
+    tail = remote(kv_ref, before_ref, tail_send, tail_recv, {"ctx": jnp.minimum(c + 1, 3)})
+
+    @pl.when(c < 3)
+    def _():
+        tail.start()
+
+    local_state = lax.dot_general(
+        kv_ref[0], kv_ref[1], (((0,), (0,)), ((), ())), preferred_element_type=jnp.float32
+    )
+    state_out[...] = local_state.astype(state_out.dtype)
+    others = [beside, across, diagonal]
+    state_copies = [
+        remote(state_out, states_in.at[c], state_send.at[way], state_recv.at[c], {"ctx": target})
+        for way, target in enumerate(others)
+    ]
+    for copy in state_copies:
+        copy.start()
+    share_along(started, z, True)
+    share_over(z)
+
+    blocks = slab_rows // row_count
+    for block in range(blocks):
+        first, end = block * row_count, (block + 1) * row_count
+        query = query_ref[first:end, :]
+        scores = lax.dot_general(
+            query, kv_ref[0, :end, :], (((1,), (1,)), ((), ())), preferred_element_type=jnp.float32
+        )
+        shape = scores.shape
+        causal = lax.broadcasted_iota(jnp.int32, shape, 1) <= first + lax.broadcasted_iota(
+            jnp.int32, shape, 0
+        )
+        inside_ref[first:end, :end] = scores
+        weights = jnp.where(causal, scores, 0.0).astype(kv_ref.dtype)
+        linear_ref[first:end, :] = jnp.dot(
+            weights, kv_ref[1, :end, :], preferred_element_type=jnp.float32
+        )
+
+    if count > 1:
+        share_stage(1)
+    for target in others:
+        remote(
+            state_out, states_in.at[target], state_send.at[0], state_recv.at[target],
+            {"ctx": beside},
+        ).wait_recv()
+    start = state_ref[...]
+    for cc in range(4):
+        start = start + jnp.where(cc < c, states_in[cc].astype(jnp.float32), 0.0)
+
+    @pl.when(c == 0)
+    def _():
+        past_copy.wait()
+
+    @pl.when(c > 0)
+    def _():
+        tail.wait_recv()
+
+    scale = 1.0 / math.sqrt(HDIM)
+
+    def head_copy(zz):
+        columns = pl.ds(pl.multiple_of(z * HDIM, HDIM), HDIM)
+        return remote(
+            heads_out.at[zz], heads_in.at[:, columns], head_send.at[zz], head_recv.at[z],
+            {"heads": zz},
+        )
+
+    for block in range(blocks):
+        first, end = block * row_count, (block + 1) * row_count
+        query = query_ref[first:end, :]
+        old = lax.dot_general(
+            query, before_ref[0, first:, :], (((1,), (1,)), ((), ())),
+            preferred_element_type=jnp.float32,
+        )
+        old_seen = lax.broadcasted_iota(jnp.int32, old.shape, 1) > lax.broadcasted_iota(
+            jnp.int32, old.shape, 0
+        )
+        old = jnp.where(old_seen, old * scale, -jnp.inf)
+        new = inside_ref[first:end, :end]
+        new_seen = lax.broadcasted_iota(jnp.int32, new.shape, 1) <= first + lax.broadcasted_iota(
+            jnp.int32, new.shape, 0
+        )
+        new = jnp.where(new_seen, new * scale, -jnp.inf)
+        top = jnp.maximum(
+            jnp.max(old, axis=-1, keepdims=True), jnp.max(new, axis=-1, keepdims=True)
+        )
+        old = jnp.exp(old - top)
+        new = jnp.exp(new - top)
+        inverse = 1.0 / (
+            jnp.sum(old, axis=-1, keepdims=True) + jnp.sum(new, axis=-1, keepdims=True)
+        )
+        window = jnp.dot(
+            (old * inverse).astype(kv_ref.dtype), before_ref[1, first:, :],
+            preferred_element_type=jnp.float32,
+        ) + jnp.dot(
+            (new * inverse).astype(kv_ref.dtype), kv_ref[1, :end, :],
+            preferred_element_type=jnp.float32,
+        )
+        linear = linear_ref[first:end, :] + jnp.dot(
+            query.astype(jnp.float32), start, precision=lax.Precision.HIGHEST,
+            preferred_element_type=jnp.float32,
+        )
+        heads_out[block] = (normalize(linear) + window).astype(heads_out.dtype)
+
+        @pl.when(block != z)
+        def _():
+            head_copy(block).start()
+
+        @pl.when(block == z)
+        def _():
+            columns = pl.ds(pl.multiple_of(z * HDIM, HDIM), HDIM)
+            heads_in[:, columns] = heads_out[block]
+
+        if block + 1 < count:
+            at_distance(block + 1, share_over)
+        if block + 2 < count:
+            share_stage(block + 2)
 
     for zz in range(count):
-        left(zz, across, 3, {"ctx": beside})
+        share_received(zz, beside)
+        share_received(zz, diagonal)
+
+        @pl.when(zz != z)
+        def _():
+            remote(
+                heads_out.at[zz], heads_in.at[:, zz * HDIM : (zz + 1) * HDIM], head_send.at[zz],
+                head_recv.at[zz], {"heads": zz},
+            ).wait_recv()
+
+    def out_tile(index, total):
+        columns = pl.ds(pl.multiple_of(index * DOT_COLUMNS, DOT_COLUMNS), DOT_COLUMNS)
+        attn = jnp.dot(heads_in[...], w_ref[:, columns], preferred_element_type=jnp.float32)
+        hidden = (tokens_ref[:, columns].astype(jnp.float32) + attn).astype(hidden_ref.dtype)
+        hidden_ref[:, columns] = hidden
+        hidden = hidden.astype(jnp.float32)
+        return total + jnp.sum(hidden * hidden, axis=-1, keepdims=True)
+
+    total = lax.fori_loop(
+        0, width // DOT_COLUMNS, out_tile, jnp.zeros((row_count, 1), jnp.float32)
+    )
+    inverse = lax.rsqrt(total / width + 1e-06)
+    for first in range(0, width, DOT_COLUMNS):
+        hidden = hidden_ref[:, first : first + DOT_COLUMNS].astype(jnp.float32)
+        normed_ref[:, first : first + DOT_COLUMNS] = (hidden * inverse).astype(normed_ref.dtype)
+
+    along(left, z, token_copy(z, True))
+    share_along(left, z, True)
+    share_relay(left, z, True)
+
+    @pl.when(c < 3)
+    def _():
+        tail.wait_send()
+
+    for copy in state_copies:
+        copy.wait_send()
+    for zz in range(count):
+        aside(left, zz, across)
+
+        @pl.when(zz != z)
+        def _():
+            along(left, zz, token_copy(zz))
+            share_along(left, zz)
+            share_relay(left, zz)
+            head_copy(zz).wait_send()
+
+
+def plan_steps(count, at, share):
+    near, far = 2 * share, 2 * (1 - share)
+    stage = near + 2 * far
+
+    def begin(place, zz):
+        return (abs(zz - place) - 1) * stage
+
+    def arrivals(place):
+        events = [(2.0, ("cross", place)), (2.0, ("side", place))]
+        ready = {(place, 0): LOAD_TIME, (place, 1): 2.1}
+        link = 2.0
+        for zz in sorted(set(range(count)) - {place}, key=lambda other: abs(other - place)):
+            first = begin(place, zz)
+            events.append((first + near, ("near", zz)))
+            events.append((first + near + far, ("far", zz)))
+            events.append((first + stage, ("cross", zz)))
+            link = max(link, first + near) + near
+            events.append((link, ("side", zz)))
+            ready[zz, 0] = first + near + far + 0.1
+            ready[zz, 1] = max(first + stage, link) + 0.1
+        return sorted(events, key=lambda event: event[0]), ready
+
+    def simulate(place):
+        events, ready = arrivals(place)
+        segments, order, now, ends, current = [], [], 0.0, {}, []
+        while ready or events:
+            while events and events[0][0] <= now + SLACK:
+                when, op = events.pop(0)
+                current.append(op)
+                zz = op[-1]
+                if op[0] == "exchange" and zz != place and place in (0, count - 1):
+                    events.append((now, ("passfar", int(zz < place), zz)))
+                    events.append((now + near + 0.3, ("passnear", int(zz < place), zz)))
+                    events.sort(key=lambda event: event[0])
+            able = [unit for unit in ready if ready[unit] <= now + SLACK]
+            if not able and not ready and not events:
+                break
+            if not able:
+                now = min([event[0] for event in events[:1]] + list(ready.values()))
+                continue
+            unit = min(able, key=lambda one: ready[one])
+            del ready[unit]
+            segments.append(current + [("pair",) + unit])
+            order.append(unit)
+            now += UNIT_TIME
+            zz, pair = unit
+            ends[zz] = ends.get(zz, 0) + 1
+            current = [("beside", zz, 1 - pair)]
+            if ends[zz] == 2:
+                events.append((now + 0.5, ("exchange", zz)))
+                events.sort(key=lambda event: event[0])
+                ends[zz] = now + 1.0
+        segments.append(current)
+        return segments, order, ends
+
+    everyone = [simulate(place) for place in range(count)]
+    segments, order, _ = everyone[at]
+    if 0 < at < count - 1:
+
+        def chain(side, zz, place, op):
+            own = everyone[place][2][zz] + (near if op == "passnear" else 0)
+            if place == side * (count - 1):
+                return own
+            hop = near if op == "passnear" else 2 * far
+            return max(own, chain(side, zz, place + 2 * side - 1, op) + hop + 0.2)
+
+        passes = [
+            (op, int(zz < at), zz)
+            for zz in range(count)
+            for op in ("passfar", "passnear")
+            if zz != at
+        ]
+        passes.sort(key=lambda one: chain(one[1], one[2], at, one[0]))
+        segments = segments[:-1] + [segments[-1] + passes]
+    return segments, order
 
 
 def expert_kernel(
@@ -244,14 +545,11 @@
     def received(zz, cc, span):
         row_copy(zz, cc, span, 0, {"ctx": beside}).wait_recv()
 
-    def along(act, zz, cc, span, own=False):
-        @pl.when(jnp.logical_and(zz >= z, z > 0))
-        def _():
-            act(row_copy(zz, cc, span, 0, {"heads": z - 1}, own))
-
-        @pl.when(jnp.logical_and(zz <= z, z < count - 1))
-        def _():
-            act(row_copy(zz, cc, span, 1, {"heads": z + 1}, own))
+    def along(act, at, zz, cc, span, own=False):
+        if zz >= at and at > 0:
+            act(row_copy(zz, cc, span, 0, {"heads": at - 1}, own))
+        if zz <= at and at < count - 1:
+            act(row_copy(zz, cc, span, 1, {"heads": at + 1}, own))
 
     def over(act, zz, cc, span, own=False):
         act(row_copy(zz, cc, span, 2, {"ctx": across}, own))
@@ -259,63 +557,43 @@
     def aside(act, zz, cc, span, own=False):
         act(row_copy(zz, cc, span, 3, {"ctx": beside}, own))
 
-    def own_sends(act, own):
+    def own_sends(act, at):
         for span in (0, 1):
-            along(act, z, c, span, own)
-            over(act, z, c, span, own)
+            along(act, at, at, c, span, True)
+            over(act, at, c, span, True)
+            aside(act, at, c, span, True)
+
+    def relays(op, at, zz, act, wait):
+        cc = c if op in ("near", "far") else across
+        span = 0 if op in ("near", "side") else 1
+        if wait:
+            received(zz, cc, span)
+        if op != "side":
+            along(act, at, zz, cc, span)
+        if op == "near":
+            over(act, zz, cc, span)
+        aside(act, zz, cc, span)
+
+    def paired(zz, pair):
         for span in (0, 1):
-            aside(act, z, c, span, own)
-
-    def own_plane_sends(act, wait):
-        for span in (1, 0):
-            if wait:
-                received(z, across, span)
-            if span == 1:
-                along(act, z, across, span)
-            aside(act, z, across, span)
-
-    def line_sends(act, wait, zz):
-        for span in (0, 1):
-            if wait:
-                received(zz, c, span)
-            along(act, zz, c, span)
-            if span == 0:
-                over(act, zz, c, span)
-            aside(act, zz, c, span)
-        if wait:
-            received(zz, across, 1)
-        along(act, zz, across, 1)
-        aside(act, zz, across, 1)
-
-    def side_sends(act, wait, zz):
-        if wait:
-            received(zz, across, 0)
-        aside(act, zz, across, 0)
-
-    def near(index):
-        index = count - 1 - index
-        more = jnp.maximum(z, count - 1 - z)
-        fewer = count - 1 - more
-        alone = more - fewer
-        paired = jnp.maximum(index - alone, 0)
-        up = jnp.where(z + more < count, more - index, index - more)
-        both = (fewer - paired // 2) * (1 - 2 * (paired % 2))
-        offset = jnp.where(index < alone, up, both)
-        return z + jnp.where(index < count - 1, offset, 0)
-
-    def compute(zz):
-        for cc in range(4):
-            row = table_ref[cc * count + zz, pl.ds(expert, 1), :]
-            scale_ref[cc * row_count : (cc + 1) * row_count, :] = jnp.broadcast_to(
+            received(zz, diagonal if pair else beside, span)
+
+    def compute(zz, pair):
+        half = jnp.where(pair == 0, c // 2, 1 - c // 2)
+        for core in range(2):
+            row = table_ref[(half * 2 + core) * count + zz, pl.ds(expert, 1), :]
+            scale_ref[core * row_count : (core + 1) * row_count, :] = jnp.broadcast_to(
                 row, (HDIM, row_count)
             ).T
 
         inner = gate_ref.shape[1]
+        rows = pl.ds(pl.multiple_of(half * 2 * row_count, 2 * row_count), 2 * row_count)
 
         def hidden_tile(index, _):
             columns = pl.ds(pl.multiple_of(index * HID_COLUMNS, HID_COLUMNS), HID_COLUMNS)
-            gate = jnp.dot(rows_ref[zz], gate_ref[:, columns], preferred_element_type=jnp.float32)
-            up = jnp.dot(rows_ref[zz], up_ref[:, columns], preferred_element_type=jnp.float32)
+            block = rows_ref[zz, rows, :]
+            gate = jnp.dot(block, gate_ref[:, columns], preferred_element_type=jnp.float32)
+            up = jnp.dot(block, up_ref[:, columns], preferred_element_type=jnp.float32)
             scale = jnp.concatenate([scale_ref[...]] * (HID_COLUMNS // HDIM), axis=1)
             hid_ref[:, columns] = (jax.nn.silu(gate) * up * scale).astype(hid_ref.dtype)
             return 0
@@ -327,7 +605,7 @@
             product = jnp.dot(
                 hid_ref[...], down_ref[:, columns], preferred_element_type=jnp.float32
             )
-            part_ref[zz, :, columns] = product.astype(part_ref.dtype)
+            part_ref[zz, rows, columns] = product.astype(part_ref.dtype)
             return 0
 
         lax.fori_loop(0, width // DOT_COLUMNS, out_tile, 0)
@@ -398,8 +676,6 @@
         return sources + ([from_across.at[zz]] if chunk == 0 else [])
 
     def exchange(zz):
-        beside_copy(0, zz).start()
-        beside_copy(1, zz).start()
         beside_copy(0, zz).wait_recv()
         add(
             to_across.at[zz],
@@ -412,164 +688,155 @@
         first, size = line_spans[chunk]
         return line_in.at[side, zz, pl.ds(first, size), :]
 
-    def starts(side):
-        return z == side * (count - 1)
-
-    def pass_line(side, zz):
-        for chunk in (1, 2, 0):
+    def starts(side, at):
+        return at == side * (count - 1)
+
+    def pass_line(at, side, zz, chunks):
+        for chunk in chunks:
             if chunk == 0:
                 across_copy(zz).wait_recv()
-
-            @pl.when(jnp.logical_not(starts(side)))
+            sources = chip_sources(zz, chunk)
+            if not starts(side, at):
+                line_copy(side, zz, chunk).wait_recv()
+                sources = sources + [line_block(side, zz, chunk)]
+            first, size = line_spans[chunk]
+            add(line_out.at[zz, pl.ds(first, size), :], sources)
+            line_copy(side, zz, chunk).start()
+
+    def perform(at, ops):
+        for op, *where in ops:
+            if op == "pair":
+                paired(*where)
+            elif op == "beside":
+                beside_copy(where[1], where[0]).start()
+            elif op == "exchange":
+                exchange(*where)
+            elif op == "passfar":
+                pass_line(at, *where, (1, 2))
+            elif op == "passnear":
+                pass_line(at, *where, (0,))
+            else:
+                relays(op, at, where[0], started, True)
+
+    def each_place(act):
+        for at in range(count):
+
+            @pl.when(z == at)
             def _():
-                line_copy(side, zz, chunk).wait_recv()
-
-            first, size = line_spans[chunk]
-            add(
-                line_out.at[zz, pl.ds(first, size), :],
-                chip_sources(zz, chunk) + [line_block(side, zz, chunk)],
-            )
-            line_copy(side, zz, chunk).start()
-
-    own_sends(started, True)
-
-    for side in (0, 1):
-
-        @pl.when(starts(side))
-        def _():
-            def clear(index, _):
-                line_in[side, index] = jnp.zeros(line_in.shape[2:], line_in.dtype)
-                return 0
-
-            lax.fori_loop(0, count, clear, 0)
+                act(at)
+
+    each_place(lambda at: own_sends(started, at))
 
     for copy in local:
         copy.wait()
-    own_plane_sends(started, True)
-
-    def distance(zz):
-        return jnp.abs(zz - z)
-
-    end_side = jnp.where(z == 0, 0, 1)
-    at_end = jnp.logical_or(z == 0, z == count - 1)
+    plans = [plan_steps(count, at, near_rows / row_count) for at in range(count)]
+    units = 2 * count
+
+    def choose(index, pick):
+        value = jnp.int32(0)
+        for at in range(count):
+            for unit in range(units):
+                here = jnp.logical_and(z == at, index == unit)
+                value = jnp.where(here, pick(plans[at][1][unit]), value)
+        return value
 
     def step(index, _):
-        zz = near(index)
-        before = near(jnp.maximum(index - 1, 0))
-        after = near(jnp.minimum(index + 1, count - 1))
-        opens = jnp.logical_and(index > 0, distance(zz) != distance(before))
-
-        @pl.when(opens)
-        def _():
-            line_sends(started, True, zz)
-
-        @pl.when(jnp.logical_and(opens, jnp.logical_and(index < count - 1, distance(after) == distance(zz))))
-        def _():
-            line_sends(started, True, after)
-
-        @pl.when(jnp.logical_and(at_end, index > 1))
-        def _():
-            pass_line(end_side, before)
-
-        @pl.when(index > 0)
-        def _():
-            side_sends(started, True, zz)
-
-        for span in (0, 1):
-            received(zz, beside, span)
-            received(zz, diagonal, span)
-        compute(zz)
-        exchange(zz)
+        def segment(at):
+            for unit in range(units):
+
+                @pl.when(index == unit)
+                def _():
+                    perform(at, plans[at][0][unit])
+
+        each_place(segment)
+        compute(choose(index, lambda unit: unit[0]), choose(index, lambda unit: unit[1]))
         return 0
 
-    lax.fori_loop(0, count, step, 0)
-
-    def link(index, _):
-        key = index // 2 + 1
-        low = z < count - 1 - z
-        side = jnp.where(low, index % 2, 1 - index % 2)
-        zz = jnp.where(side == 0, key, count - 1 - key)
-        valid = jnp.where(side == 0, zz > z, zz < z)
-        done = jnp.logical_and(starts(side), key < count - 1)
-
-        @pl.when(jnp.logical_and(valid, jnp.logical_not(done)))
-        def _():
-            pass_line(side, zz)
-
-        return 0
-
-    lax.fori_loop(0, 2 * (count - 1), link, 0)
-
-    def both_sides(chunk):
-        for side in (0, 1):
-
-            @pl.when(jnp.logical_not(starts(side)))
-            def _():
-                line_copy(side, z, chunk).wait_recv()
-
-        return [line_block(side, z, chunk) for side in (0, 1)]
-
-    sides = both_sides(2)
-    add(last_out, chip_sources(z, 2) + sides)
-    last_copy().start()
-    across_copy(z).wait_recv()
-    sides = both_sides(0)
-    add(
-        out_ref.at[pl.ds(0, near_rows), :],
-        [hidden_ref.at[pl.ds(0, near_rows), :]] + chip_sources(z, 0) + sides,
-    )
-    sides = both_sides(1)
-    last_copy().wait_recv()
-    add(
-        out_ref.at[pl.ds(near_rows, far_rows), :],
-        [hidden_ref.at[pl.ds(near_rows, far_rows), :]] + chip_sources(z, 1) + sides + [last_in],
-    )
-
-    last_copy().wait_send()
-    own_sends(left, True)
-    own_plane_sends(left, False)
-
-    def drain(zz, _):
-        beside_copy(0, zz).wait_send()
-        beside_copy(1, zz).wait_send()
-        across_copy(zz).wait_send()
-
-        @pl.when(zz != z)
-        def _():
-            line_sends(left, False, zz)
-            side_sends(left, False, zz)
-            side = jnp.where(zz > z, 0, 1)
-            for chunk in range(3):
-                line_copy(side, zz, chunk).wait_send()
-
-        return 0
-
-    lax.fori_loop(0, count, drain, 0)
-
-
-def gather_blocks(kinds, operands, collective_id, name):
-    count, ctx_count = lax.axis_size("heads"), lax.axis_size("ctx")
-    slots = [count if kind == "line" else count * ctx_count for kind in kinds]
-    shapes = [
-        (value.shape[0] // ctx_count if kind == "share" else value.shape[0], value.shape[1])
-        for kind, value in zip(kinds, operands)
-    ]
+    lax.fori_loop(0, units, step, 0)
+    each_place(lambda at: perform(at, plans[at][0][units]))
+
+    def finish(at):
+        sides = [side for side in (0, 1) if not starts(side, at)]
+
+        def arrived(chunk):
+            for side in sides:
+                line_copy(side, at, chunk).wait_recv()
+            return chip_sources(at, chunk) + [line_block(side, at, chunk) for side in sides]
+
+        add(last_out, arrived(2))
+        last_copy().start()
+        across_copy(at).wait_recv()
+        for chunk, (first, size) in enumerate(spans):
+            rows = pl.ds(first, size)
+            sources = arrived(chunk)
+            if chunk == 1:
+                last_copy().wait_recv()
+                sources = sources + [last_in]
+            add(out_ref.at[rows, :], [hidden_ref.at[rows, :]] + sources)
+        last_copy().wait_send()
+        own_sends(left, at)
+        relays("side", at, at, left, False)
+        relays("cross", at, at, left, False)
+        for zz in range(count):
+            beside_copy(0, zz).wait_send()
+            beside_copy(1, zz).wait_send()
+            across_copy(zz).wait_send()
+            if zz != at:
+                for op in ("near", "far", "cross", "side"):
+                    relays(op, at, zz, left, False)
+                for chunk in range(3):
+                    line_copy(int(zz < at), zz, chunk).wait_send()
+
+    each_place(finish)
+
+
+def attend(tokens, w_out, table, state_in, past_kv, w_qkv):
+    count = lax.axis_size("heads")
+    row_count, width = tokens.shape
+    slab_rows = count * row_count
+    kind = tokens.dtype
+    slots = 4 * count
+    dma = pltpu.SemaphoreType.DMA
+    vmem, anywhere = pl.BlockSpec(memory_space=pltpu.VMEM), pl.BlockSpec(memory_space=pl.ANY)
     return pl.pallas_call(
-        functools.partial(gather_kernel, count, kinds),
+        functools.partial(attend_kernel, count),
         out_shape=[
-            jax.ShapeDtypeStruct((slot,) + shape, value.dtype)
-            for slot, shape, value in zip(slots, shapes, operands)
+            jax.ShapeDtypeStruct((row_count, width), kind),
+            jax.ShapeDtypeStruct((row_count, width), kind),
+            jax.ShapeDtypeStruct((slots,) + table.shape, table.dtype),
         ],
-        in_specs=[pl.BlockSpec(memory_space=pltpu.VMEM)] * len(kinds),
-        out_specs=[pl.BlockSpec(memory_space=pl.ANY)] * len(kinds),
-        scratch_shapes=[pltpu.SemaphoreType.DMA((4, slot)) for slot in slots]
-        + [pltpu.SemaphoreType.DMA((slot,)) for slot in slots]
-        + [pltpu.SemaphoreType.DMA((len(kinds),))],
+        in_specs=[vmem, anywhere, vmem, vmem, anywhere, anywhere],
+        out_specs=[vmem, vmem, anywhere],
+        scratch_shapes=[
+            pltpu.VMEM((count, row_count, width), kind),
+            pltpu.VMEM((width, 3 * HDIM), kind),
+            pltpu.VMEM((count * HDIM, width), kind),
+            pltpu.VMEM((slab_rows, HDIM), kind),
+            pltpu.VMEM((2, slab_rows, HDIM), kind),
+            pltpu.VMEM((2, WINDOW, HDIM), kind),
+            pltpu.VMEM((slab_rows, slab_rows), jnp.float32),
+            pltpu.VMEM((slab_rows, HDIM), jnp.float32),
+            pltpu.VMEM((HDIM, HDIM), kind),
+            pltpu.VMEM((4, HDIM, HDIM), kind),
+            pltpu.VMEM((count, row_count, HDIM), kind),
+            pltpu.VMEM((row_count, count * HDIM), kind),
+            dma((7,)),
+            dma((2, count)),
+            dma((count,)),
+            dma((2, 4, slots)),
+            dma((2, slots)),
+            dma(()),
+            dma(()),
+            dma((3,)),
+            dma((4,)),
+            dma((count,)),
+            dma((count,)),
+        ],
         compiler_params=pltpu.CompilerParams(
-            collective_id=collective_id, has_side_effects=True
+            collective_id=2, has_side_effects=True, vmem_limit_bytes=FRONT_BYTES
         ),
-        name=name,
-    )(*operands)
+        name="attend",
+    )(tokens, w_out, table, state_in, past_kv, w_qkv)
 
 
 def near_share(row_count):
@@ -593,8 +860,8 @@
         scratch_shapes=[
             pltpu.VMEM((count, 4 * row_count, width), kind),
             pltpu.VMEM((count, 4 * row_count, width), kind),
-            pltpu.VMEM((4 * row_count, inner), kind),
-            pltpu.VMEM((4 * row_count, HDIM), jnp.float32),
+            pltpu.VMEM((2 * row_count, inner), kind),
+            pltpu.VMEM((2 * row_count, HDIM), jnp.float32),
             pltpu.VMEM(w_gate.shape, kind),
             pltpu.VMEM(w_up.shape, kind),
             pltpu.VMEM(w_down.shape, kind),
@@ -629,20 +896,12 @@
     return jnp.sum(jnp.where(chosen, gate_weights[:, :, None], 0.0), axis=1).T
 
 
-def gather_inputs(tokens, w_out, table):
-    slab, w_rows, tables = gather_blocks(
-        ("line", "share", "group"), (tokens, w_out, table), 2, "gather_inputs"
-    )
-    return slab.reshape(-1, tokens.shape[1]), w_rows.reshape(-1, w_out.shape[1]), tables
-
-
 def on_device(
     tokens, state_in, past_kv, w_qkv, w_out, w_gate, w_up, w_down, expert_ids, gate_weights
 ):
     row_count, model_width = tokens.shape
     inner_width = w_qkv.shape[2]
     local_heads = inner_width // HDIM
-    w_flat = w_qkv.reshape(model_width, 3 * inner_width)
     ctx_count = lax.axis_size("ctx")
     head_count = lax.axis_size("heads")
     exp_local = w_gate.shape[0]
@@ -654,20 +913,23 @@
         ctx_count == 4
         and exp_local == 1
         and row_count % HDIM == 0
-        and w_out.shape[0] % 64 == 0
+        and local_heads == 1
+        and head_count * row_count == WINDOW
         and w_gate.shape[2] % HID_COLUMNS == 0
         and row_count * devices <= expert_count * capacity
     )
     if dense:
         table = expert_table(expert_ids, gate_weights, expert_count)
-        slab, w_rows, tables = gather_inputs(tokens, w_out, table)
-    else:
-        slab, w_rows = [
-            lax.all_gather(value, "heads", axis=0, tiled=True) for value in (tokens, w_out)
-        ]
+        hidden_state, normed, tables = attend(
+            tokens, w_out, table, state_in[0], past_kv, jnp.transpose(w_qkv, (1, 0, 2))
+        )
+        return run_experts(hidden_state, normed, tables, w_gate[0], w_up[0], w_down[0])
+    slab, w_rows = [
+        lax.all_gather(value, "heads", axis=0, tiled=True) for value in (tokens, w_out)
+    ]
     projected = jnp.dot(
         slab,
-        w_flat,
+        w_qkv.reshape(model_width, 3 * inner_width),
         preferred_element_type=jnp.float32,
     ).astype(jnp.bfloat16)
     slab_rows = projected.shape[0]
@@ -730,8 +992,6 @@
     hidden_state = (tokens.astype(jnp.float32) + attn).astype(jnp.bfloat16)
     hidden_float = hidden_state.astype(jnp.float32)
     normed = normalize(hidden_float).astype(jnp.bfloat16)
-    if dense:
-        return run_experts(hidden_state, normed, tables, w_gate[0], w_up[0], w_down[0])
     picks = expert_ids.reshape(-1)
     onehot = (picks[:, None] == jnp.arange(expert_count, dtype=jnp.int32)[None, :]).astype(
         jnp.int32

time: 223 us -> 187 us (0.84)
  blocking collectives: 14.5 us -> 0 us
  Pallas kernels: 193 us -> 184 us
  matrix products: 5.39 us -> 0 us
  starting transfers between devices: 2.5 us -> 0 us
    pallas_call x1, Pallas kernels: 134 us -> 114 us  [run_experts(): pl.pallas_call(functools.partial(expert_kernel, count, near_rows), out_sh...]
    pallas_call x1, Pallas kernels: 60 us -> 69.7 us  [attend(): pl.pallas_call(functools.partial(attend_kernel, count), out_shape=[jax.Sh...]
    all_to_all x1 -> x0, blocking collectives: 9.05 us -> none  [on_device(): lax.all_to_all(heads_out, 'heads', split_axis=0, concat_axis=1, tiled=True)]
    all_gather x1 -> x0, blocking collectives: 5.42 us -> none  [entering(): gathered = lax.all_gather(x.astype(jnp.bfloat16), axis)]
    dot_general x7 -> x0, matrix products: 5.39 us -> none  [the longest x1 2.6 us: on_device(): jnp.dot(slab, w_flat, preferred_element_type=jnp.float32)]
    ppermute x1 -> x0, starting transfers between devices: 2.5 us -> none  [from_behind(): return lax.ppermute(block, axis, route)]
  transfers between devices with their start and end apart: 1 -> 0, of which waited for: 0 -> 0; matrix products, arithmetic and copies ran while one was open for 0% -> 0% of each run, Pallas kernels for 0% -> 0%
where the time goes in v2:
time: 187 us
  Pallas kernels  184 us (98%)
  local copies, waits for them, and re-layouts  1.88 us (1%)
    pallas_call x1, Pallas kernels, run_experts(): pl.pallas_call(functools.partial(expert_kernel, count, near_rows), out_sh...  114 us
    pallas_call x1, Pallas kernels, attend(): pl.pallas_call(functools.partial(attend_kernel, count), out_shape=[jax.Sh...  69.7 us

profile of v2, /device:TPU:0, one launch (start us, length us, event | category | flops | bytes accessed | tf_op | source)
XLA Modules:
  0.0 187.1 jit_solution(18030777267446427117)
XLA Ops:
  0.0 1.3 select_reduce_fusion
  1.3 69.7 %attend.1 = (bf16[128,2048]{1,0:T(8,128)(2,1)}, bf16[128,2048]{1,0:T(8,128)(2,1)}, f32[16,16,128]{2,1,0:T(8,128)}) custom-call(bf16[128,2048]{1,0:T(8,128)(2,1)} %tokens_ref.1, bf16[128,2048]{1,0:T(8,128)(2,1)} %share_hbm.1, f32[16,128]{1,0:T(8,128)} %bitcast.11, f32[128,128]{1,0:T(8,128)} %bitcast.10, bf16[2,512,128]{2,1,0:T(8,128)(2,1)} %past_hbm.1, ...), custom_call_target="tpu_custom_call" | custom-call | tf_op jit(solution)/shard_map/attend/pallas_call | solution.py:801
  71.1 114.2 %run_experts.1 = bf16[128,2048]{1,0:T(8,128)(2,1)} custom-call(bf16[128,2048]{1,0:T(8,128)(2,1)} %get-tuple-element.8.hidden_ref, bf16[128,2048]{1,0:T(8,128)(2,1)} %get-tuple-element.9.own_ref, f32[16,16,128]{2,1,0:T(8,128)} %get-tuple-element.10.table_ref, bf16[2048,768]{1,0:T(8,128)(2,1)} %bitcast.6, bf16[2048,768]{1,0:T(8,128)(2,1)} %bitcast.7, ...), custom_call_target="tpu_custom_call" | custom-call | tf_op jit(solution)/shard_map/run_experts/pallas_call | solution.py:855
  185.2 1.9 %copy.14 = bf16[128,2048]{1,0:T(8,128)(2,1)} copy(bf16[128,2048]{1,0:T(8,128)(2,1)} %run_experts.1) | data formatting | bytes 1048576

commit v3 on v2

--- a/solution.py
+++ b/solution.py
@@ -43,6 +43,29 @@
 UNIT_TIME = 0.75
 SLACK = 0.05
 NEAR_EIGHTHS = 5
+SUM_EIGHTHS = 5
+OWN_LINE, OWN_OVER, OWN_ASIDE, LOAD, NEAR, FAR, CROSS, SIDE = range(8)
+COMPUTE, EXCHANGE, LINE, FINISH, BESIDE, PASS_FAR, PASS_NEAR, PAIR = range(8, 16)
+STEPS = (
+    (
+        (OWN_LINE, 0), (OWN_OVER, 1), (LOAD,), (CROSS, 0), (NEAR, 1), (OWN_OVER, 0), (NEAR, 2), (CROSS, 1),
+        (OWN_LINE, 1), (SIDE, 1), (COMPUTE, 1, 1), (NEAR, 3), (FAR, 1), (SIDE, 0), (COMPUTE, 1, 0), (SIDE, 3),
+        (CROSS, 3), (EXCHANGE, 1), (LINE, 0, 1, 2), (LINE, 0, 1, 1), (FAR, 3), (COMPUTE, 3, 1), (COMPUTE, 3, 0),
+        (EXCHANGE, 3), (CROSS, 2), (LINE, 0, 3, 2), (LINE, 0, 3, 1), (SIDE, 2), (FAR, 2), (COMPUTE, 2, 0),
+        (OWN_ASIDE,), (LINE, 0, 3, 0), (COMPUTE, 2, 1), (EXCHANGE, 2), (LINE, 0, 2, 2), (COMPUTE, 0, 0),
+        (LINE, 0, 2, 1), (COMPUTE, 0, 1), (LINE, 0, 2, 0), (EXCHANGE, 0), (FINISH, 2), (LINE, 0, 1, 0), (FINISH, 1),
+        (FINISH, 0),
+    ),
+    (
+        (OWN_OVER, 1), (OWN_OVER, 0), (OWN_LINE, 0), (NEAR, 0), (CROSS, 1), (NEAR, 2), (NEAR, 3), (CROSS, 0),
+        (OWN_LINE, 1), (LOAD,), (SIDE, 2), (SIDE, 1), (SIDE, 0), (OWN_ASIDE,), (FAR, 0), (CROSS, 3),
+        (FAR, 3), (FAR, 2), (COMPUTE, 0, 1), (CROSS, 2), (SIDE, 3), (COMPUTE, 0, 0), (COMPUTE, 3, 1),
+        (COMPUTE, 3, 0), (EXCHANGE, 3), (COMPUTE, 2, 0), (LINE, 0, 3, 2), (EXCHANGE, 0), (COMPUTE, 2, 1),
+        (LINE, 0, 3, 1), (COMPUTE, 1, 1), (EXCHANGE, 2), (LINE, 1, 0, 1), (LINE, 0, 3, 0), (COMPUTE, 1, 0),
+        (LINE, 1, 0, 2), (LINE, 0, 2, 2), (LINE, 1, 0, 0), (LINE, 0, 2, 1), (EXCHANGE, 1), (FINISH, 2),
+        (LINE, 0, 2, 0), (FINISH, 1), (FINISH, 0),
+    ),
+)
 
 
 def place(count):
@@ -202,13 +225,10 @@
         def _():
             act(z + distance)
 
-    def share_stage(distance):
-        def one(zz):
-            share_received(zz, c)
-            share_along(started, zz)
-            share_relay(started, zz)
-
-        at_distance(distance, one)
+    def share_onward(zz):
+        share_received(zz, c)
+        share_along(started, zz)
+        share_relay(started, zz)
 
     def share_over(zz):
         share_received(zz, across)
@@ -247,6 +267,17 @@
             token_relay(after)
 
         project(zz)
+        alone = jnp.logical_and(index > 0, jnp.logical_not(jnp.logical_and(opens, double)))
+        distance = jnp.abs(zz - z)
+
+        @pl.when(jnp.logical_and(alone, distance == 1))
+        def _():
+            share_along(started, z, True)
+
+        @pl.when(jnp.logical_and(alone, distance > 1))
+        def _():
+            at_distance(distance - 1, share_onward)
+
         return 0
 
     lax.fori_loop(0, count, step, 0)
@@ -268,7 +299,6 @@
     ]
     for copy in state_copies:
         copy.start()
-    share_along(started, z, True)
     share_over(z)
 
     blocks = slab_rows // row_count
@@ -288,8 +318,6 @@
             weights, kv_ref[1, :end, :], preferred_element_type=jnp.float32
         )
 
-    if count > 1:
-        share_stage(1)
     for target in others:
         remote(
             state_out, states_in.at[target], state_send.at[0], state_recv.at[target],
@@ -362,10 +390,10 @@
             columns = pl.ds(pl.multiple_of(z * HDIM, HDIM), HDIM)
             heads_in[:, columns] = heads_out[block]
 
+        if block == 0:
+            at_distance(jnp.maximum(z, count - 1 - z), share_onward)
         if block + 1 < count:
             at_distance(block + 1, share_over)
-        if block + 2 < count:
-            share_stage(block + 2)
 
     for zz in range(count):
         share_received(zz, beside)
@@ -423,16 +451,16 @@
         return (abs(zz - place) - 1) * stage
 
     def arrivals(place):
-        events = [(2.0, ("cross", place)), (2.0, ("side", place))]
+        events = [(2.0, (CROSS, place)), (2.0, (SIDE, place))]
         ready = {(place, 0): LOAD_TIME, (place, 1): 2.1}
         link = 2.0
         for zz in sorted(set(range(count)) - {place}, key=lambda other: abs(other - place)):
             first = begin(place, zz)
-            events.append((first + near, ("near", zz)))
-            events.append((first + near + far, ("far", zz)))
-            events.append((first + stage, ("cross", zz)))
+            events.append((first + near, (NEAR, zz)))
+            events.append((first + near + far, (FAR, zz)))
+            events.append((first + stage, (CROSS, zz)))
             link = max(link, first + near) + near
-            events.append((link, ("side", zz)))
+            events.append((link, (SIDE, zz)))
             ready[zz, 0] = first + near + far + 0.1
             ready[zz, 1] = max(first + stage, link) + 0.1
         return sorted(events, key=lambda event: event[0]), ready
@@ -445,9 +473,9 @@
                 when, op = events.pop(0)
                 current.append(op)
                 zz = op[-1]
-                if op[0] == "exchange" and zz != place and place in (0, count - 1):
-                    events.append((now, ("passfar", int(zz < place), zz)))
-                    events.append((now + near + 0.3, ("passnear", int(zz < place), zz)))
+                if op[0] == EXCHANGE and zz != place and place in (0, count - 1):
+                    events.append((now, (PASS_FAR, int(zz < place), zz)))
+                    events.append((now + near + 0.3, (PASS_NEAR, int(zz < place), zz)))
                     events.sort(key=lambda event: event[0])
             able = [unit for unit in ready if ready[unit] <= now + SLACK]
             if not able and not ready and not events:
@@ -457,14 +485,14 @@
                 continue
             unit = min(able, key=lambda one: ready[one])
             del ready[unit]
-            segments.append(current + [("pair",) + unit])
+            segments.append(current + [(PAIR,) + unit])
             order.append(unit)
             now += UNIT_TIME
             zz, pair = unit
             ends[zz] = ends.get(zz, 0) + 1
-            current = [("beside", zz, 1 - pair)]
+            current = [(BESIDE, zz, 1 - pair)]
             if ends[zz] == 2:
-                events.append((now + 0.5, ("exchange", zz)))
+                events.append((now + 0.5, (EXCHANGE, zz)))
                 events.sort(key=lambda event: event[0])
                 ends[zz] = now + 1.0
         segments.append(current)
@@ -475,25 +503,55 @@
     if 0 < at < count - 1:
 
         def chain(side, zz, place, op):
-            own = everyone[place][2][zz] + (near if op == "passnear" else 0)
+            own = everyone[place][2][zz] + (near if op == PASS_NEAR else 0)
             if place == side * (count - 1):
                 return own
-            hop = near if op == "passnear" else 2 * far
+            hop = near if op == PASS_NEAR else 2 * far
             return max(own, chain(side, zz, place + 2 * side - 1, op) + hop + 0.2)
 
         passes = [
             (op, int(zz < at), zz)
             for zz in range(count)
-            for op in ("passfar", "passnear")
+            for op in (PASS_FAR, PASS_NEAR)
             if zz != at
         ]
         passes.sort(key=lambda one: chain(one[1], one[2], at, one[0]))
         segments = segments[:-1] + [segments[-1] + passes]
-    return segments, order
+    steps = [(OWN_LINE, 0), (OWN_OVER, 0), (OWN_ASIDE,), (OWN_LINE, 1), (OWN_OVER, 1), (LOAD,)]
+    for index, ops in enumerate(segments):
+        for op, *where in ops:
+            if op == EXCHANGE:
+                steps.append((EXCHANGE, *where))
+            elif op == PASS_FAR:
+                steps += [(LINE, *where, 1), (LINE, *where, 2)]
+            elif op == PASS_NEAR:
+                steps.append((LINE, *where, 0))
+            elif op not in (PAIR, BESIDE):
+                steps.append((op, *where))
+        if index < len(order):
+            steps.append((COMPUTE,) + order[index])
+    return steps + [(FINISH, 2), (FINISH, 0), (FINISH, 1)]
+
+
+def mirrored(step, count):
+    op, *where = step
+    if op in (NEAR, FAR, CROSS, SIDE, EXCHANGE, COMPUTE):
+        return (op, count - 1 - where[0], *where[1:])
+    if op == LINE:
+        return (op, 1 - where[0], count - 1 - where[1], where[2])
+    return step
+
+
+def steps_of(count, at, share):
+    if count != len(STEPS) * 2:
+        return plan_steps(count, at, share)
+    if at < len(STEPS):
+        return list(STEPS[at])
+    return [mirrored(step, count) for step in STEPS[count - 1 - at]]
 
 
 def expert_kernel(
-    count, near_rows, hidden_ref, own_ref, table_ref, gate_hbm, up_hbm, down_hbm, out_ref,
+    count, near_rows, sum_rows, hidden_ref, own_ref, table_ref, gate_hbm, up_hbm, down_hbm, out_ref,
     rows_ref, part_ref, hid_ref, scale_ref, gate_ref, up_ref, down_ref,
     from_beside, to_across, from_across, line_out, line_in, last_out, last_in,
     local_sem, row_send, row_recv, beside_send, beside_recv, across_send, across_recv,
@@ -503,6 +561,7 @@
     row_count, width = own_ref.shape
     far_rows = row_count - near_rows
     spans = [(0, near_rows), (near_rows, far_rows)]
+    sum_spans = [(0, sum_rows), (sum_rows, row_count - sum_rows)]
     expert = c * count + z
     local = [
         pltpu.make_async_copy(source, target, local_sem.at[index])
@@ -557,20 +616,14 @@
     def aside(act, zz, cc, span, own=False):
         act(row_copy(zz, cc, span, 3, {"ctx": beside}, own))
 
-    def own_sends(act, at):
-        for span in (0, 1):
-            along(act, at, at, c, span, True)
-            over(act, at, c, span, True)
-            aside(act, at, c, span, True)
-
     def relays(op, at, zz, act, wait):
-        cc = c if op in ("near", "far") else across
-        span = 0 if op in ("near", "side") else 1
+        cc = c if op in (NEAR, FAR) else across
+        span = 0 if op in (NEAR, SIDE) else 1
         if wait:
             received(zz, cc, span)
-        if op != "side":
+        if op != SIDE:
             along(act, at, zz, cc, span)
-        if op == "near":
+        if op == NEAR:
             over(act, zz, cc, span)
         aside(act, zz, cc, span)
 
@@ -631,7 +684,7 @@
             device_id_type=MESH,
         )
 
-    line_spans = [(0, near_rows), (near_rows, far_rows), (row_count, far_rows)]
+    line_spans = sum_spans + [(row_count, row_count - sum_rows)]
 
     def line_copy(side, zz, chunk):
         first, size = line_spans[chunk]
@@ -667,23 +720,14 @@
 
     def chip_sources(zz, chunk):
         cc, kind = (across, 0) if chunk == 2 else (c, 1)
-        span = 0 if chunk == 0 else 1
-        first, size = spans[span]
+        first, size = sum_spans[0 if chunk == 0 else 1]
+        start = pl.multiple_of(cc * row_count + first, 16)
         sources = [
-            part_ref.at[zz, window(cc, span), :],
+            part_ref.at[zz, pl.ds(start, size), :],
             from_beside.at[kind, zz, pl.ds(first, size), :],
         ]
         return sources + ([from_across.at[zz]] if chunk == 0 else [])
 
-    def exchange(zz):
-        beside_copy(0, zz).wait_recv()
-        add(
-            to_across.at[zz],
-            [part_ref.at[zz, window(across, 0), :], from_beside.at[0, zz, pl.ds(0, near_rows), :]],
-        )
-        across_copy(zz).start()
-        beside_copy(1, zz).wait_recv()
-
     def line_block(side, zz, chunk):
         first, size = line_spans[chunk]
         return line_in.at[side, zz, pl.ds(first, size), :]
@@ -691,30 +735,72 @@
     def starts(side, at):
         return at == side * (count - 1)
 
-    def pass_line(at, side, zz, chunks):
-        for chunk in chunks:
+    def perform(at, steps, waited):
+        waited = set(waited)
+
+        def once(make, *key):
+            if key not in waited:
+                waited.add(key)
+                make().wait_recv()
+
+        def ready(zz, chunk):
+            kind = 0 if chunk == 2 else 1
+            once(lambda: beside_copy(kind, zz), kind, zz)
             if chunk == 0:
-                across_copy(zz).wait_recv()
-            sources = chip_sources(zz, chunk)
-            if not starts(side, at):
-                line_copy(side, zz, chunk).wait_recv()
-                sources = sources + [line_block(side, zz, chunk)]
-            first, size = line_spans[chunk]
-            add(line_out.at[zz, pl.ds(first, size), :], sources)
-            line_copy(side, zz, chunk).start()
-
-    def perform(at, ops):
-        for op, *where in ops:
-            if op == "pair":
+                once(lambda: across_copy(zz), 2, zz)
+            return chip_sources(zz, chunk)
+
+        def arrived(zz, chunk, sides):
+            sources = ready(zz, chunk)
+            for side in sides:
+                if not starts(side, at):
+                    line_copy(side, zz, chunk).wait_recv()
+                    sources = sources + [line_block(side, zz, chunk)]
+            return sources
+
+        for op, *where in steps:
+            if op == OWN_LINE:
+                along(started, at, at, c, where[0], True)
+            elif op == OWN_OVER:
+                over(started, at, c, where[0], True)
+            elif op == OWN_ASIDE:
+                for span in (0, 1):
+                    aside(started, at, c, span, True)
+            elif op == LOAD:
+                for copy in local:
+                    copy.wait()
+            elif op == COMPUTE:
                 paired(*where)
-            elif op == "beside":
+            elif op == BESIDE:
                 beside_copy(where[1], where[0]).start()
-            elif op == "exchange":
-                exchange(*where)
-            elif op == "passfar":
-                pass_line(at, *where, (1, 2))
-            elif op == "passnear":
-                pass_line(at, *where, (0,))
+            elif op == EXCHANGE:
+                zz = where[0]
+                once(lambda: beside_copy(0, zz), 0, zz)
+                start = pl.multiple_of(across * row_count, row_count)
+                add(
+                    to_across.at[zz],
+                    [
+                        part_ref.at[zz, pl.ds(start, sum_rows), :],
+                        from_beside.at[0, zz, pl.ds(0, sum_rows), :],
+                    ],
+                )
+                across_copy(zz).start()
+            elif op == LINE:
+                side, zz, chunk = where
+                first, size = line_spans[chunk]
+                add(line_out.at[zz, pl.ds(first, size), :], arrived(zz, chunk, (side,)))
+                line_copy(side, zz, chunk).start()
+            elif op == FINISH and where[0] == 2:
+                add(last_out, arrived(at, 2, (0, 1)))
+                last_copy().start()
+            elif op == FINISH:
+                first, size = sum_spans[where[0]]
+                rows = pl.ds(first, size)
+                sources = arrived(at, where[0], (0, 1))
+                if where[0] == 1:
+                    last_copy().wait_recv()
+                    sources = sources + [last_in]
+                add(out_ref.at[rows, :], [hidden_ref.at[rows, :]] + sources)
             else:
                 relays(op, at, where[0], started, True)
 
@@ -725,19 +811,40 @@
             def _():
                 act(at)
 
-    each_place(lambda at: own_sends(started, at))
-
-    for copy in local:
-        copy.wait()
-    plans = [plan_steps(count, at, near_rows / row_count) for at in range(count)]
     units = 2 * count
+    segments, orders = [], []
+    for at in range(count):
+        parts, order = [[]], []
+        for one in steps_of(count, at, near_rows / row_count):
+            parts[-1].append(one)
+            if one[0] == COMPUTE:
+                zz, pair = one[1:]
+                order.append((zz, pair))
+                parts.append([(BESIDE, zz, 1 - pair)])
+        segments.append(parts)
+        orders.append(order)
+
+    def waits_of(at, unit):
+        keys = set()
+        for one in sum(segments[at][:unit], []):
+            zz, chunk = at, one[-1]
+            if one[0] == EXCHANGE:
+                zz, chunk = one[1], 2
+            elif one[0] == LINE:
+                zz = one[2]
+            elif one[0] != FINISH:
+                continue
+            keys.add((0 if chunk == 2 else 1, zz))
+            if chunk == 0:
+                keys.add((2, zz))
+        return keys
 
     def choose(index, pick):
         value = jnp.int32(0)
         for at in range(count):
             for unit in range(units):
                 here = jnp.logical_and(z == at, index == unit)
-                value = jnp.where(here, pick(plans[at][1][unit]), value)
+                value = jnp.where(here, pick(orders[at][unit]), value)
         return value
 
     def step(index, _):
@@ -746,43 +853,29 @@
 
                 @pl.when(index == unit)
                 def _():
-                    perform(at, plans[at][0][unit])
+                    perform(at, segments[at][unit], waits_of(at, unit))
 
         each_place(segment)
         compute(choose(index, lambda unit: unit[0]), choose(index, lambda unit: unit[1]))
         return 0
 
     lax.fori_loop(0, units, step, 0)
-    each_place(lambda at: perform(at, plans[at][0][units]))
 
     def finish(at):
-        sides = [side for side in (0, 1) if not starts(side, at)]
-
-        def arrived(chunk):
-            for side in sides:
-                line_copy(side, at, chunk).wait_recv()
-            return chip_sources(at, chunk) + [line_block(side, at, chunk) for side in sides]
-
-        add(last_out, arrived(2))
-        last_copy().start()
-        across_copy(at).wait_recv()
-        for chunk, (first, size) in enumerate(spans):
-            rows = pl.ds(first, size)
-            sources = arrived(chunk)
-            if chunk == 1:
-                last_copy().wait_recv()
-                sources = sources + [last_in]
-            add(out_ref.at[rows, :], [hidden_ref.at[rows, :]] + sources)
+        perform(at, segments[at][units], waits_of(at, units))
         last_copy().wait_send()
-        own_sends(left, at)
-        relays("side", at, at, left, False)
-        relays("cross", at, at, left, False)
+        for span in (0, 1):
+            along(left, at, at, c, span, True)
+            over(left, at, c, span, True)
+            aside(left, at, c, span, True)
+        relays(SIDE, at, at, left, False)
+        relays(CROSS, at, at, left, False)
         for zz in range(count):
             beside_copy(0, zz).wait_send()
             beside_copy(1, zz).wait_send()
             across_copy(zz).wait_send()
             if zz != at:
-                for op in ("near", "far", "cross", "side"):
+                for op in (NEAR, FAR, CROSS, SIDE):
                     relays(op, at, zz, left, False)
                 for chunk in range(3):
                     line_copy(int(zz < at), zz, chunk).wait_send()
@@ -839,21 +932,22 @@
     )(tokens, w_out, table, state_in, past_kv, w_qkv)
 
 
-def near_share(row_count):
-    return max(16, row_count * NEAR_EIGHTHS // 8 // 16 * 16)
+def near_share(row_count, eighths):
+    return max(16, row_count * eighths // 8 // 16 * 16)
 
 
 def run_experts(hidden, normed, tables, w_gate, w_up, w_down):
     count = lax.axis_size("heads")
     row_count, width = normed.shape
     inner = w_gate.shape[1]
-    near_rows = near_share(row_count)
-    far_rows = row_count - near_rows
+    near_rows = near_share(row_count, NEAR_EIGHTHS)
+    sum_rows = near_share(row_count, SUM_EIGHTHS)
+    far_rows = row_count - sum_rows
     dma = pltpu.SemaphoreType.DMA
     kind = normed.dtype
     vmem, anywhere = pl.BlockSpec(memory_space=pltpu.VMEM), pl.BlockSpec(memory_space=pl.ANY)
     return pl.pallas_call(
-        functools.partial(expert_kernel, count, near_rows),
+        functools.partial(expert_kernel, count, near_rows, sum_rows),
         out_shape=jax.ShapeDtypeStruct((row_count, width), kind),
         in_specs=[vmem] * 3 + [anywhere] * 3,
         out_specs=vmem,
@@ -866,8 +960,8 @@
             pltpu.VMEM(w_up.shape, kind),
             pltpu.VMEM(w_down.shape, kind),
             pltpu.VMEM((2, count, row_count, width), kind),
-            pltpu.VMEM((count, near_rows, width), kind),
-            pltpu.VMEM((count, near_rows, width), kind),
+            pltpu.VMEM((count, sum_rows, width), kind),
+            pltpu.VMEM((count, sum_rows, width), kind),
             pltpu.VMEM((count, row_count + far_rows, width), kind),
             pltpu.VMEM((2, count, row_count + far_rows, width), kind),
             pltpu.VMEM((far_rows, width), kind),

time: 187 us -> 168 us (0.90); the launches traced: 187 us -> 165 us
  Pallas kernels: 184 us -> 162 us
    pallas_call x1, Pallas kernels: 114 us -> 94.3 us  [run_experts(): pl.pallas_call(functools.partial(expert_kernel, count, near_rows, sum_row...]
    pallas_call x1, Pallas kernels: 69.7 us -> 67.2 us  [attend(): pl.pallas_call(functools.partial(attend_kernel, count), out_shape=[jax.Sh...]
where the time goes in v3:
time: 168 us; the launch traced here: 165 us
  Pallas kernels  162 us (96%)
  local copies, waits for them, and re-layouts  1.88 us (1%)
    pallas_call x1, Pallas kernels, run_experts(): pl.pallas_call(functools.partial(expert_kernel, count, near_rows, sum_row...  94.3 us
    pallas_call x1, Pallas kernels, attend(): pl.pallas_call(functools.partial(attend_kernel, count), out_shape=[jax.Sh...  67.2 us

profile of v3, /device:TPU:0, one launch (start us, length us, event | category | flops | bytes accessed | tf_op | source)
XLA Modules:
  0.0 164.7 jit_solution(303044256722091281)
XLA Ops:
  0.0 1.3 select_reduce_fusion
  1.3 67.2 %attend.1 = (bf16[128,2048]{1,0:T(8,128)(2,1)}, bf16[128,2048]{1,0:T(8,128)(2,1)}, f32[16,16,128]{2,1,0:T(8,128)}) custom-call(bf16[128,2048]{1,0:T(8,128)(2,1)} %tokens_ref.1, bf16[128,2048]{1,0:T(8,128)(2,1)} %share_hbm.1, f32[16,128]{1,0:T(8,128)} %bitcast.11, f32[128,128]{1,0:T(8,128)} %bitcast.10, bf16[2,512,128]{2,1,0:T(8,128)(2,1)} %past_hbm.1, ...), custom_call_target="tpu_custom_call" | custom-call | tf_op jit(solution)/shard_map/attend/pallas_call | solution.py:894
  68.5 94.3 %run_experts.1 = bf16[128,2048]{1,0:T(8,128)(2,1)} custom-call(bf16[128,2048]{1,0:T(8,128)(2,1)} %get-tuple-element.8.hidden_ref, bf16[128,2048]{1,0:T(8,128)(2,1)} %get-tuple-element.9.own_ref, f32[16,16,128]{2,1,0:T(8,128)} %get-tuple-element.10.table_ref, bf16[2048,768]{1,0:T(8,128)(2,1)} %bitcast.6, bf16[2048,768]{1,0:T(8,128)(2,1)} %bitcast.7, ...), custom_call_target="tpu_custom_call" | custom-call | tf_op jit(solution)/shard_map/run_experts/pallas_call | solution.py:949
  162.9 1.9 %copy.14 = bf16[128,2048]{1,0:T(8,128)(2,1)} copy(bf16[128,2048]{1,0:T(8,128)(2,1)} %run_experts.1) | data formatting | bytes 1048576

commit v4 on v3

--- a/solution.py
+++ b/solution.py
@@ -39,31 +39,39 @@
 ADD_ROWS = 16
 DOT_COLUMNS = 512
 HID_COLUMNS = 256
-LOAD_TIME = 0.6
-UNIT_TIME = 0.75
-SLACK = 0.05
-NEAR_EIGHTHS = 5
-SUM_EIGHTHS = 5
-OWN_LINE, OWN_OVER, OWN_ASIDE, LOAD, NEAR, FAR, CROSS, SIDE = range(8)
-COMPUTE, EXCHANGE, LINE, FINISH, BESIDE, PASS_FAR, PASS_NEAR, PAIR = range(8, 16)
+SPANS = ((32, 0), (32, 0), (32, 0), (32, 1))
+OWN_LINE, OWN_OVER, OWN_ASIDE, LOAD, ROWS, CROSS = range(6)
+COMPUTE, EXCHANGE, LINE, FINISH, BESIDE = range(6, 11)
 STEPS = (
     (
-        (OWN_LINE, 0), (OWN_OVER, 1), (LOAD,), (CROSS, 0), (NEAR, 1), (OWN_OVER, 0), (NEAR, 2), (CROSS, 1),
-        (OWN_LINE, 1), (SIDE, 1), (COMPUTE, 1, 1), (NEAR, 3), (FAR, 1), (SIDE, 0), (COMPUTE, 1, 0), (SIDE, 3),
-        (CROSS, 3), (EXCHANGE, 1), (LINE, 0, 1, 2), (LINE, 0, 1, 1), (FAR, 3), (COMPUTE, 3, 1), (COMPUTE, 3, 0),
-        (EXCHANGE, 3), (CROSS, 2), (LINE, 0, 3, 2), (LINE, 0, 3, 1), (SIDE, 2), (FAR, 2), (COMPUTE, 2, 0),
-        (OWN_ASIDE,), (LINE, 0, 3, 0), (COMPUTE, 2, 1), (EXCHANGE, 2), (LINE, 0, 2, 2), (COMPUTE, 0, 0),
-        (LINE, 0, 2, 1), (COMPUTE, 0, 1), (LINE, 0, 2, 0), (EXCHANGE, 0), (FINISH, 2), (LINE, 0, 1, 0), (FINISH, 1),
-        (FINISH, 0),
+        (OWN_LINE, 1), (OWN_OVER, 0), (OWN_OVER, 1), (OWN_LINE, 2), (LOAD,), (OWN_ASIDE,), (OWN_OVER, 3),
+        (OWN_LINE, 0), (ROWS, 1, 0), (OWN_LINE, 3), (ROWS, 1, 2), (OWN_OVER, 2), (CROSS, 0, 3), (COMPUTE, 0, 0),
+        (ROWS, 1, 3), (ROWS, 3, 1), (CROSS, 1, 2), (ROWS, 1, 1), (COMPUTE, 1, 0), (CROSS, 1, 0), (ROWS, 3, 2),
+        (CROSS, 1, 1), (CROSS, 3, 1), (CROSS, 1, 3), (CROSS, 0, 0), (ROWS, 3, 0), (CROSS, 3, 2), (ROWS, 2, 2),
+        (CROSS, 0, 2), (COMPUTE, 1, 1), (LINE, 0, 1, 3, 0), (CROSS, 3, 3), (CROSS, 3, 0), (EXCHANGE, 1, 2),
+        (ROWS, 3, 3), (LINE, 0, 1, 3, 1), (COMPUTE, 3, 1), (ROWS, 2, 0), (LINE, 0, 1, 2, 0), (ROWS, 2, 1),
+        (COMPUTE, 3, 0), (LINE, 0, 3, 3, 1), (EXCHANGE, 3, 1), (EXCHANGE, 3, 2), (CROSS, 2, 3), (EXCHANGE, 3, 0),
+        (ROWS, 2, 3), (EXCHANGE, 1, 0), (CROSS, 2, 0), (CROSS, 2, 2), (CROSS, 2, 1), (LINE, 0, 3, 3, 0),
+        (COMPUTE, 2, 0), (LINE, 0, 3, 1, 0), (EXCHANGE, 1, 1), (LINE, 0, 3, 2, 0), (COMPUTE, 2, 1),
+        (LINE, 0, 2, 3, 0), (CROSS, 0, 1), (EXCHANGE, 2, 0), (EXCHANGE, 2, 1), (LINE, 0, 3, 0, 0), (LINE, 0, 2, 3, 1),
+        (EXCHANGE, 2, 2), (COMPUTE, 0, 1), (LINE, 0, 2, 0, 0), (EXCHANGE, 0, 1), (EXCHANGE, 0, 0), (LINE, 0, 2, 1, 0),
+        (LINE, 0, 2, 2, 0), (LINE, 0, 1, 1, 0), (EXCHANGE, 0, 2), (FINISH, 3, 1), (LINE, 0, 1, 0, 0), (FINISH, 2, 0),
+        (FINISH, 1, 0), (FINISH, 0, 0), (FINISH, 3, 0),
     ),
     (
-        (OWN_OVER, 1), (OWN_OVER, 0), (OWN_LINE, 0), (NEAR, 0), (CROSS, 1), (NEAR, 2), (NEAR, 3), (CROSS, 0),
-        (OWN_LINE, 1), (LOAD,), (SIDE, 2), (SIDE, 1), (SIDE, 0), (OWN_ASIDE,), (FAR, 0), (CROSS, 3),
-        (FAR, 3), (FAR, 2), (COMPUTE, 0, 1), (CROSS, 2), (SIDE, 3), (COMPUTE, 0, 0), (COMPUTE, 3, 1),
-        (COMPUTE, 3, 0), (EXCHANGE, 3), (COMPUTE, 2, 0), (LINE, 0, 3, 2), (EXCHANGE, 0), (COMPUTE, 2, 1),
-        (LINE, 0, 3, 1), (COMPUTE, 1, 1), (EXCHANGE, 2), (LINE, 1, 0, 1), (LINE, 0, 3, 0), (COMPUTE, 1, 0),
-        (LINE, 1, 0, 2), (LINE, 0, 2, 2), (LINE, 1, 0, 0), (LINE, 0, 2, 1), (EXCHANGE, 1), (FINISH, 2),
-        (LINE, 0, 2, 0), (FINISH, 1), (FINISH, 0),
+        (OWN_ASIDE,), (OWN_LINE, 0), (OWN_OVER, 3), (OWN_OVER, 0), (OWN_LINE, 2), (ROWS, 0, 1), (OWN_LINE, 3),
+        (ROWS, 0, 2), (OWN_LINE, 1), (ROWS, 3, 1), (ROWS, 2, 2), (ROWS, 0, 0), (LOAD,), (CROSS, 0, 3), (ROWS, 0, 3),
+        (ROWS, 3, 2), (CROSS, 1, 3), (COMPUTE, 1, 0), (ROWS, 3, 0), (OWN_OVER, 1), (CROSS, 0, 2), (CROSS, 0, 1),
+        (CROSS, 0, 0), (COMPUTE, 0, 0), (CROSS, 1, 0), (CROSS, 3, 3), (ROWS, 3, 3), (ROWS, 2, 0), (CROSS, 3, 2),
+        (ROWS, 2, 1), (CROSS, 3, 0), (COMPUTE, 0, 1), (OWN_OVER, 2), (CROSS, 2, 3), (CROSS, 3, 1), (CROSS, 2, 2),
+        (COMPUTE, 3, 0), (EXCHANGE, 0, 0), (CROSS, 2, 1), (EXCHANGE, 0, 2), (ROWS, 2, 3), (CROSS, 2, 0),
+        (COMPUTE, 3, 1), (CROSS, 1, 1), (COMPUTE, 2, 1), (EXCHANGE, 0, 1), (CROSS, 1, 2), (COMPUTE, 2, 0),
+        (LINE, 0, 3, 3, 1), (EXCHANGE, 3, 1), (EXCHANGE, 3, 2), (LINE, 0, 3, 3, 0), (COMPUTE, 1, 1), (EXCHANGE, 3, 0),
+        (LINE, 0, 3, 1, 0), (LINE, 0, 3, 2, 0), (EXCHANGE, 2, 1), (LINE, 0, 2, 3, 0), (LINE, 1, 0, 3, 1),
+        (EXCHANGE, 2, 2), (EXCHANGE, 2, 0), (LINE, 1, 0, 2, 0), (EXCHANGE, 1, 2), (LINE, 0, 3, 0, 0),
+        (LINE, 1, 0, 1, 0), (LINE, 0, 2, 3, 1), (LINE, 1, 0, 3, 0), (LINE, 1, 0, 0, 0), (LINE, 0, 2, 0, 0),
+        (EXCHANGE, 1, 1), (FINISH, 3, 1), (LINE, 0, 2, 1, 0), (EXCHANGE, 1, 0), (LINE, 0, 2, 2, 0), (FINISH, 1, 0),
+        (FINISH, 3, 0), (FINISH, 2, 0), (FINISH, 0, 0),
     ),
 )
 
@@ -247,6 +255,17 @@
         kv_ref[0, rows, :] = product[:, HDIM : 2 * HDIM]
         kv_ref[1, rows, :] = product[:, 2 * HDIM :]
 
+        @pl.when(c < 3)
+        def _():
+            tail_copy(zz).start()
+
+    def tail_copy(zz):
+        rows = rows_of(zz, row_count)
+        return remote(
+            kv_ref.at[:, rows, :], before_ref.at[:, rows, :], tail_send.at[zz], tail_recv.at[zz],
+            {"ctx": jnp.minimum(c + 1, 3)},
+        )
+
     def token_relay(zz):
         token_copy(zz)(0, {"heads": z - 1}).wait_recv()
         along(started, zz, token_copy(zz))
@@ -281,12 +300,6 @@
         return 0
 
     lax.fori_loop(0, count, step, 0)
-
-    tail = remote(kv_ref, before_ref, tail_send, tail_recv, {"ctx": jnp.minimum(c + 1, 3)})
-
-    @pl.when(c < 3)
-    def _():
-        tail.start()
 
     local_state = lax.dot_general(
         kv_ref[0], kv_ref[1], (((0,), (0,)), ((), ())), preferred_element_type=jnp.float32
@@ -333,7 +346,8 @@
 
     @pl.when(c > 0)
     def _():
-        tail.wait_recv()
+        for zz in range(count):
+            tail_copy(zz).wait_recv()
 
     scale = 1.0 / math.sqrt(HDIM)
 
@@ -428,7 +442,8 @@
 
     @pl.when(c < 3)
     def _():
-        tail.wait_send()
+        for zz in range(count):
+            tail_copy(zz).wait_send()
 
     for copy in state_copies:
         copy.wait_send()
@@ -443,115 +458,54 @@
             head_copy(zz).wait_send()
 
 
-def plan_steps(count, at, share):
-    near, far = 2 * share, 2 * (1 - share)
-    stage = near + 2 * far
-
-    def begin(place, zz):
-        return (abs(zz - place) - 1) * stage
-
-    def arrivals(place):
-        events = [(2.0, (CROSS, place)), (2.0, (SIDE, place))]
-        ready = {(place, 0): LOAD_TIME, (place, 1): 2.1}
-        link = 2.0
-        for zz in sorted(set(range(count)) - {place}, key=lambda other: abs(other - place)):
-            first = begin(place, zz)
-            events.append((first + near, (NEAR, zz)))
-            events.append((first + near + far, (FAR, zz)))
-            events.append((first + stage, (CROSS, zz)))
-            link = max(link, first + near) + near
-            events.append((link, (SIDE, zz)))
-            ready[zz, 0] = first + near + far + 0.1
-            ready[zz, 1] = max(first + stage, link) + 0.1
-        return sorted(events, key=lambda event: event[0]), ready
-
-    def simulate(place):
-        events, ready = arrivals(place)
-        segments, order, now, ends, current = [], [], 0.0, {}, []
-        while ready or events:
-            while events and events[0][0] <= now + SLACK:
-                when, op = events.pop(0)
-                current.append(op)
-                zz = op[-1]
-                if op[0] == EXCHANGE and zz != place and place in (0, count - 1):
-                    events.append((now, (PASS_FAR, int(zz < place), zz)))
-                    events.append((now + near + 0.3, (PASS_NEAR, int(zz < place), zz)))
-                    events.sort(key=lambda event: event[0])
-            able = [unit for unit in ready if ready[unit] <= now + SLACK]
-            if not able and not ready and not events:
-                break
-            if not able:
-                now = min([event[0] for event in events[:1]] + list(ready.values()))
-                continue
-            unit = min(able, key=lambda one: ready[one])
-            del ready[unit]
-            segments.append(current + [(PAIR,) + unit])
-            order.append(unit)
-            now += UNIT_TIME
-            zz, pair = unit
-            ends[zz] = ends.get(zz, 0) + 1
-            current = [(BESIDE, zz, 1 - pair)]
-            if ends[zz] == 2:
-                events.append((now + 0.5, (EXCHANGE, zz)))
-                events.sort(key=lambda event: event[0])
-                ends[zz] = now + 1.0
-        segments.append(current)
-        return segments, order, ends
-
-    everyone = [simulate(place) for place in range(count)]
-    segments, order, _ = everyone[at]
-    if 0 < at < count - 1:
-
-        def chain(side, zz, place, op):
-            own = everyone[place][2][zz] + (near if op == PASS_NEAR else 0)
-            if place == side * (count - 1):
-                return own
-            hop = near if op == PASS_NEAR else 2 * far
-            return max(own, chain(side, zz, place + 2 * side - 1, op) + hop + 0.2)
-
-        passes = [
-            (op, int(zz < at), zz)
-            for zz in range(count)
-            for op in (PASS_FAR, PASS_NEAR)
-            if zz != at
-        ]
-        passes.sort(key=lambda one: chain(one[1], one[2], at, one[0]))
-        segments = segments[:-1] + [segments[-1] + passes]
-    steps = [(OWN_LINE, 0), (OWN_OVER, 0), (OWN_ASIDE,), (OWN_LINE, 1), (OWN_OVER, 1), (LOAD,)]
-    for index, ops in enumerate(segments):
-        for op, *where in ops:
-            if op == EXCHANGE:
-                steps.append((EXCHANGE, *where))
-            elif op == PASS_FAR:
-                steps += [(LINE, *where, 1), (LINE, *where, 2)]
-            elif op == PASS_NEAR:
-                steps.append((LINE, *where, 0))
-            elif op not in (PAIR, BESIDE):
-                steps.append((op, *where))
-        if index < len(order):
-            steps.append((COMPUTE,) + order[index])
-    return steps + [(FINISH, 2), (FINISH, 0), (FINISH, 1)]
+def plain_steps(count, at):
+    spans = range(len(SPANS))
+    steps = [(OWN_LINE, span) for span in spans] + [(OWN_OVER, span) for span in spans]
+    steps += [(OWN_ASIDE,), (LOAD,)]
+    for distance in range(count):
+        planes = sorted({at - distance, at + distance} & set(range(count)))
+        for op in (ROWS, CROSS):
+            if op == CROSS or distance:
+                steps += [(op, zz, span) for zz in planes for span in reversed(spans)]
+        steps += [(COMPUTE, zz, pair) for zz in planes for pair in (0, 1)]
+    near = [span for span in spans if not SPANS[span][1]]
+    far = [span for span in spans if SPANS[span][1]]
+    steps += [(EXCHANGE, zz, span) for zz in range(count) for span in near]
+    for key in range(1, count):
+        links = [(0, key)] * (key > at) + [(1, count - 1 - key)] * (count - 1 - key < at)
+        for link in links if at < count - 1 - at else reversed(links):
+            steps += [(LINE, *link, span, 0) for span in spans]
+            steps += [(LINE, *link, span, 1) for span in far]
+    return steps + [(FINISH, span, 1) for span in far] + [(FINISH, span, 0) for span in spans]
 
 
 def mirrored(step, count):
     op, *where = step
-    if op in (NEAR, FAR, CROSS, SIDE, EXCHANGE, COMPUTE):
-        return (op, count - 1 - where[0], *where[1:])
+    if op in (ROWS, CROSS, EXCHANGE, COMPUTE):
+        return (op, count - 1 - where[0], where[1])
     if op == LINE:
-        return (op, 1 - where[0], count - 1 - where[1], where[2])
+        return (op, 1 - where[0], count - 1 - where[1], *where[2:])
     return step
 
 
-def steps_of(count, at, share):
+def steps_of(count, at):
     if count != len(STEPS) * 2:
-        return plan_steps(count, at, share)
+        return plain_steps(count, at)
     if at < len(STEPS):
         return list(STEPS[at])
     return [mirrored(step, count) for step in STEPS[count - 1 - at]]
 
 
+def span_rows(row_count):
+    spans, first = [], 0
+    for share, far in SPANS:
+        spans.append((first, row_count * share // 128, far))
+        first += row_count * share // 128
+    return spans, sum(size for _, size, far in spans if far)
+
+
 def expert_kernel(
-    count, near_rows, sum_rows, hidden_ref, own_ref, table_ref, gate_hbm, up_hbm, down_hbm, out_ref,
+    count, hidden_ref, own_ref, table_ref, gate_hbm, up_hbm, down_hbm, out_ref,
     rows_ref, part_ref, hid_ref, scale_ref, gate_ref, up_ref, down_ref,
     from_beside, to_across, from_across, line_out, line_in, last_out, last_in,
     local_sem, row_send, row_recv, beside_send, beside_recv, across_send, across_recv,
@@ -559,9 +513,8 @@
 ):
     z, c, beside, across, diagonal = place(count)
     row_count, width = own_ref.shape
-    far_rows = row_count - near_rows
-    spans = [(0, near_rows), (near_rows, far_rows)]
-    sum_spans = [(0, sum_rows), (sum_rows, row_count - sum_rows)]
+    spans, far_rows = span_rows(row_count)
+    near_rows = row_count - far_rows
     expert = c * count + z
     local = [
         pltpu.make_async_copy(source, target, local_sem.at[index])
@@ -579,11 +532,11 @@
     greet(z, count, beside, across)
 
     def window(cc, span):
-        first, size = spans[span]
+        first, size, _ = spans[span]
         return pl.ds(pl.multiple_of(cc * row_count + first, 16), size)
 
     def row_copy(zz, cc, span, way, target, own=False):
-        first, size = spans[span]
+        first, size, _ = spans[span]
         slot = zz * 4 + cc
         block = rows_ref.at[zz, window(cc, span), :]
         return pltpu.make_async_remote_copy(
@@ -616,19 +569,19 @@
     def aside(act, zz, cc, span, own=False):
         act(row_copy(zz, cc, span, 3, {"ctx": beside}, own))
 
-    def relays(op, at, zz, act, wait):
-        cc = c if op in (NEAR, FAR) else across
-        span = 0 if op in (NEAR, SIDE) else 1
+    def relays(op, at, zz, span, act, wait):
+        cc = c if op == ROWS else across
+        far = spans[span][2]
         if wait:
             received(zz, cc, span)
-        if op != SIDE:
+        if op == ROWS or far:
             along(act, at, zz, cc, span)
-        if op == NEAR:
+        if op == ROWS and not far:
             over(act, zz, cc, span)
         aside(act, zz, cc, span)
 
     def paired(zz, pair):
-        for span in (0, 1):
+        for span in range(len(spans)):
             received(zz, diagonal if pair else beside, span)
 
     def compute(zz, pair):
@@ -674,35 +627,41 @@
             device_id_type=MESH,
         )
 
-    def across_copy(zz):
+    def across_copy(zz, span):
+        first, size, _ = spans[span]
         return pltpu.make_async_remote_copy(
-            src_ref=to_across.at[zz],
-            dst_ref=from_across.at[zz],
-            send_sem=across_send.at[zz],
-            recv_sem=across_recv.at[zz],
+            src_ref=to_across.at[zz, pl.ds(first, size), :],
+            dst_ref=from_across.at[zz, pl.ds(first, size), :],
+            send_sem=across_send.at[span, zz],
+            recv_sem=across_recv.at[span, zz],
             device_id={"ctx": across},
             device_id_type=MESH,
         )
 
-    line_spans = sum_spans + [(row_count, row_count - sum_rows)]
-
-    def line_copy(side, zz, chunk):
-        first, size = line_spans[chunk]
+    def line_rows(span, other):
+        first, size, _ = spans[span]
+        return pl.ds(row_count + first - near_rows if other else first, size)
+
+    def line_copy(side, zz, span, other):
         return pltpu.make_async_remote_copy(
-            src_ref=line_out.at[zz, pl.ds(first, size), :],
-            dst_ref=line_in.at[side, zz, pl.ds(first, size), :],
-            send_sem=line_send.at[chunk, zz],
-            recv_sem=line_recv.at[chunk, side, zz],
+            src_ref=line_out.at[zz, line_rows(span, other), :],
+            dst_ref=line_in.at[side, zz, line_rows(span, other), :],
+            send_sem=line_send.at[2 * span + other, zz],
+            recv_sem=line_recv.at[2 * span + other, side, zz],
             device_id={"heads": z + 1 - 2 * side},
             device_id_type=MESH,
         )
 
-    def last_copy():
+    def last_rows(span):
+        first, size, _ = spans[span]
+        return pl.ds(first - near_rows, size)
+
+    def last_copy(span):
         return pltpu.make_async_remote_copy(
-            src_ref=last_out,
-            dst_ref=last_in,
-            send_sem=last_send,
-            recv_sem=last_recv,
+            src_ref=last_out.at[last_rows(span), :],
+            dst_ref=last_in.at[last_rows(span), :],
+            send_sem=last_send.at[span],
+            recv_sem=last_recv.at[span],
             device_id={"ctx": across},
             device_id_type=MESH,
         )
@@ -718,44 +677,37 @@
 
         lax.fori_loop(0, target.shape[0] // ADD_ROWS, chunk, 0)
 
-    def chip_sources(zz, chunk):
-        cc, kind = (across, 0) if chunk == 2 else (c, 1)
-        first, size = sum_spans[0 if chunk == 0 else 1]
-        start = pl.multiple_of(cc * row_count + first, 16)
+    def starts(side, at):
+        return at == side * (count - 1)
+
+    def chip_sources(zz, span, other):
+        first, size, far = spans[span]
+        start = pl.multiple_of((across if other else c) * row_count + first, 16)
         sources = [
             part_ref.at[zz, pl.ds(start, size), :],
-            from_beside.at[kind, zz, pl.ds(first, size), :],
+            from_beside.at[1 - other, zz, pl.ds(first, size), :],
         ]
-        return sources + ([from_across.at[zz]] if chunk == 0 else [])
-
-    def line_block(side, zz, chunk):
-        first, size = line_spans[chunk]
-        return line_in.at[side, zz, pl.ds(first, size), :]
-
-    def starts(side, at):
-        return at == side * (count - 1)
+        if not far and not other:
+            sources.append(from_across.at[zz, pl.ds(first, size), :])
+        return sources
 
     def perform(at, steps, waited):
         waited = set(waited)
 
-        def once(make, *key):
-            if key not in waited:
-                waited.add(key)
-                make().wait_recv()
-
-        def ready(zz, chunk):
-            kind = 0 if chunk == 2 else 1
-            once(lambda: beside_copy(kind, zz), kind, zz)
-            if chunk == 0:
-                once(lambda: across_copy(zz), 2, zz)
-            return chip_sources(zz, chunk)
-
-        def arrived(zz, chunk, sides):
-            sources = ready(zz, chunk)
+        def once(kind, zz):
+            if (kind, zz) not in waited:
+                waited.add((kind, zz))
+                beside_copy(kind, zz).wait_recv()
+
+        def arrived(zz, span, other, sides):
+            once(1 - other, zz)
+            if not spans[span][2]:
+                across_copy(zz, span).wait_recv()
+            sources = chip_sources(zz, span, other)
             for side in sides:
                 if not starts(side, at):
-                    line_copy(side, zz, chunk).wait_recv()
-                    sources = sources + [line_block(side, zz, chunk)]
+                    line_copy(side, zz, span, other).wait_recv()
+                    sources.append(line_in.at[side, zz, line_rows(span, other), :])
             return sources
 
         for op, *where in steps:
@@ -764,7 +716,7 @@
             elif op == OWN_OVER:
                 over(started, at, c, where[0], True)
             elif op == OWN_ASIDE:
-                for span in (0, 1):
+                for span in range(len(spans)):
                     aside(started, at, c, span, True)
             elif op == LOAD:
                 for copy in local:
@@ -774,35 +726,37 @@
             elif op == BESIDE:
                 beside_copy(where[1], where[0]).start()
             elif op == EXCHANGE:
-                zz = where[0]
-                once(lambda: beside_copy(0, zz), 0, zz)
-                start = pl.multiple_of(across * row_count, row_count)
+                zz, span = where
+                once(0, zz)
+                first, size, _ = spans[span]
+                start = pl.multiple_of(across * row_count + first, 16)
                 add(
-                    to_across.at[zz],
+                    to_across.at[zz, pl.ds(first, size), :],
                     [
-                        part_ref.at[zz, pl.ds(start, sum_rows), :],
-                        from_beside.at[0, zz, pl.ds(0, sum_rows), :],
+                        part_ref.at[zz, pl.ds(start, size), :],
+                        from_beside.at[0, zz, pl.ds(first, size), :],
                     ],
                 )
-                across_copy(zz).start()
+                across_copy(zz, span).start()
             elif op == LINE:
-                side, zz, chunk = where
-                first, size = line_spans[chunk]
-                add(line_out.at[zz, pl.ds(first, size), :], arrived(zz, chunk, (side,)))
-                line_copy(side, zz, chunk).start()
-            elif op == FINISH and where[0] == 2:
-                add(last_out, arrived(at, 2, (0, 1)))
-                last_copy().start()
+                side, zz, span, other = where
+                add(line_out.at[zz, line_rows(span, other), :], arrived(zz, span, other, (side,)))
+                line_copy(side, zz, span, other).start()
+            elif op == FINISH and where[1]:
+                span = where[0]
+                add(last_out.at[last_rows(span), :], arrived(at, span, 1, (0, 1)))
+                last_copy(span).start()
             elif op == FINISH:
-                first, size = sum_spans[where[0]]
+                span = where[0]
+                first, size, far = spans[span]
                 rows = pl.ds(first, size)
-                sources = arrived(at, where[0], (0, 1))
-                if where[0] == 1:
-                    last_copy().wait_recv()
-                    sources = sources + [last_in]
+                sources = arrived(at, span, 0, (0, 1))
+                if far:
+                    last_copy(span).wait_recv()
+                    sources.append(last_in.at[last_rows(span), :])
                 add(out_ref.at[rows, :], [hidden_ref.at[rows, :]] + sources)
             else:
-                relays(op, at, where[0], started, True)
+                relays(op, at, *where, started, True)
 
     def each_place(act):
         for at in range(count):
@@ -815,7 +769,7 @@
     segments, orders = [], []
     for at in range(count):
         parts, order = [[]], []
-        for one in steps_of(count, at, near_rows / row_count):
+        for one in steps_of(count, at):
             parts[-1].append(one)
             if one[0] == COMPUTE:
                 zz, pair = one[1:]
@@ -826,17 +780,13 @@
 
     def waits_of(at, unit):
         keys = set()
-        for one in sum(segments[at][:unit], []):
-            zz, chunk = at, one[-1]
-            if one[0] == EXCHANGE:
-                zz, chunk = one[1], 2
-            elif one[0] == LINE:
-                zz = one[2]
-            elif one[0] != FINISH:
-                continue
-            keys.add((0 if chunk == 2 else 1, zz))
-            if chunk == 0:
-                keys.add((2, zz))
+        for op, *where in sum(segments[at][:unit], []):
+            if op == EXCHANGE:
+                keys.add((0, where[0]))
+            elif op == LINE:
+                keys.add((1 - where[3], where[1]))
+            elif op == FINISH:
+                keys.add((1 - where[1], at))
         return keys
 
     def choose(index, pick):
@@ -863,22 +813,23 @@
 
     def finish(at):
         perform(at, segments[at][units], waits_of(at, units))
-        last_copy().wait_send()
-        for span in (0, 1):
+        for span, (_, _, far) in enumerate(spans):
+            if far:
+                last_copy(span).wait_send()
             along(left, at, at, c, span, True)
             over(left, at, c, span, True)
             aside(left, at, c, span, True)
-        relays(SIDE, at, at, left, False)
-        relays(CROSS, at, at, left, False)
+            for zz in range(count):
+                relays(CROSS, at, zz, span, left, False)
+                if not far:
+                    across_copy(zz, span).wait_send()
+                if zz != at:
+                    relays(ROWS, at, zz, span, left, False)
+                    for other in range(1 + far):
+                        line_copy(int(zz < at), zz, span, other).wait_send()
         for zz in range(count):
             beside_copy(0, zz).wait_send()
             beside_copy(1, zz).wait_send()
-            across_copy(zz).wait_send()
-            if zz != at:
-                for op in (NEAR, FAR, CROSS, SIDE):
-                    relays(op, at, zz, left, False)
-                for chunk in range(3):
-                    line_copy(int(zz < at), zz, chunk).wait_send()
 
     each_place(finish)
 
@@ -918,8 +869,8 @@
             dma((count,)),
             dma((2, 4, slots)),
             dma((2, slots)),
-            dma(()),
-            dma(()),
+            dma((count,)),
+            dma((count,)),
             dma((3,)),
             dma((4,)),
             dma((count,)),
@@ -932,22 +883,18 @@
     )(tokens, w_out, table, state_in, past_kv, w_qkv)
 
 
-def near_share(row_count, eighths):
-    return max(16, row_count * eighths // 8 // 16 * 16)
-
-
 def run_experts(hidden, normed, tables, w_gate, w_up, w_down):
     count = lax.axis_size("heads")
     row_count, width = normed.shape
     inner = w_gate.shape[1]
-    near_rows = near_share(row_count, NEAR_EIGHTHS)
-    sum_rows = near_share(row_count, SUM_EIGHTHS)
-    far_rows = row_count - sum_rows
+    far_rows = span_rows(row_count)[1]
+    near_rows = row_count - far_rows
+    cuts = len(SPANS)
     dma = pltpu.SemaphoreType.DMA
     kind = normed.dtype
     vmem, anywhere = pl.BlockSpec(memory_space=pltpu.VMEM), pl.BlockSpec(memory_space=pl.ANY)
     return pl.pallas_call(
-        functools.partial(expert_kernel, count, near_rows, sum_rows),
+        functools.partial(expert_kernel, count),
         out_shape=jax.ShapeDtypeStruct((row_count, width), kind),
         in_specs=[vmem] * 3 + [anywhere] * 3,
         out_specs=vmem,
@@ -960,23 +907,23 @@
             pltpu.VMEM(w_up.shape, kind),
             pltpu.VMEM(w_down.shape, kind),
             pltpu.VMEM((2, count, row_count, width), kind),
-            pltpu.VMEM((count, sum_rows, width), kind),
-            pltpu.VMEM((count, sum_rows, width), kind),
+            pltpu.VMEM((count, near_rows, width), kind),
+            pltpu.VMEM((count, near_rows, width), kind),
             pltpu.VMEM((count, row_count + far_rows, width), kind),
             pltpu.VMEM((2, count, row_count + far_rows, width), kind),
             pltpu.VMEM((far_rows, width), kind),
             pltpu.VMEM((far_rows, width), kind),
             dma((4,)),
-            dma((4, 2, 4 * count)),
-            dma((2, 4 * count)),
+            dma((4, cuts, 4 * count)),
+            dma((cuts, 4 * count)),
             dma((2, count)),
             dma((2, count)),
-            dma((count,)),
-            dma((count,)),
-            dma((3, count)),
-            dma((3, 2, count)),
-            dma(()),
-            dma(()),
+            dma((cuts, count)),
+            dma((cuts, count)),
+            dma((2 * cuts, count)),
+            dma((2 * cuts, 2, count)),
+            dma((cuts,)),
+            dma((cuts,)),
         ],
         compiler_params=pltpu.CompilerParams(
             collective_id=0, has_side_effects=True, vmem_limit_bytes=VMEM_BYTES

time: 168 us -> 159 us (0.946); the launches traced: 165 us -> 159 us
  Pallas kernels: 162 us -> 155 us
    pallas_call x1, Pallas kernels: 94.3 us -> 89.3 us  [run_experts(): pl.pallas_call(functools.partial(expert_kernel, count), out_shape=jax.Sha...]
where the time goes in v4:
time: 159 us
  Pallas kernels  155 us (97%)
  local copies, waits for them, and re-layouts  1.88 us (1%)
    pallas_call x1, Pallas kernels, run_experts(): pl.pallas_call(functools.partial(expert_kernel, count), out_shape=jax.Sha...  89.3 us
    pallas_call x1, Pallas kernels, attend(): pl.pallas_call(functools.partial(attend_kernel, count), out_shape=[jax.Sh...  66 us

profile of v4, /device:TPU:0, one launch (start us, length us, event | category | flops | bytes accessed | tf_op | source)
XLA Modules:
  0.0 158.5 jit_solution(9656261033163200235)
XLA Ops:
  0.0 1.3 select_reduce_fusion
  1.3 66.0 %attend.1 = (bf16[128,2048]{1,0:T(8,128)(2,1)}, bf16[128,2048]{1,0:T(8,128)(2,1)}, f32[16,16,128]{2,1,0:T(8,128)}) custom-call(bf16[128,2048]{1,0:T(8,128)(2,1)} %tokens_ref.1, bf16[128,2048]{1,0:T(8,128)(2,1)} %share_hbm.1, f32[16,128]{1,0:T(8,128)} %bitcast.11, f32[128,128]{1,0:T(8,128)} %bitcast.10, bf16[2,512,128]{2,1,0:T(8,128)(2,1)} %past_hbm.1, ...), custom_call_target="tpu_custom_call" | custom-call | tf_op jit(solution)/shard_map/attend/pallas_call | solution.py:845
  67.3 89.3 %run_experts.1 = bf16[128,2048]{1,0:T(8,128)(2,1)} custom-call(bf16[128,2048]{1,0:T(8,128)(2,1)} %get-tuple-element.8.hidden_ref, bf16[128,2048]{1,0:T(8,128)(2,1)} %get-tuple-element.9.own_ref, f32[16,16,128]{2,1,0:T(8,128)} %get-tuple-element.10.table_ref, bf16[2048,768]{1,0:T(8,128)(2,1)} %bitcast.6, bf16[2048,768]{1,0:T(8,128)(2,1)} %bitcast.7, ...), custom_call_target="tpu_custom_call" | custom-call | tf_op jit(solution)/shard_map/run_experts/pallas_call | solution.py:896
  156.6 1.9 %copy.14 = bf16[128,2048]{1,0:T(8,128)(2,1)} copy(bf16[128,2048]{1,0:T(8,128)(2,1)} %run_experts.1) | data formatting | bytes 1048576

commit v5 on v4

--- a/solution.py
+++ b/solution.py
@@ -34,9 +34,9 @@
 
 
 MESH = pl.DeviceIdType.MESH
-VMEM_BYTES = 60 * 1024 * 1024
-FRONT_BYTES = 60 * 1024 * 1024
+VMEM_BYTES = 62 * 1024 * 1024
 ADD_ROWS = 16
+PIECES = 2
 DOT_COLUMNS = 512
 HID_COLUMNS = 256
 SPANS = ((32, 0), (32, 0), (32, 0), (32, 1))
@@ -85,26 +85,6 @@
     return z, c, beside, across, diagonal
 
 
-def greet(z, count, beside, across):
-    barrier = pltpu.get_barrier_semaphore()
-
-    def signal(target):
-        pl.semaphore_signal(barrier, inc=1, device_id=target, device_id_type=MESH)
-
-    signal({"ctx": beside})
-    signal({"ctx": across})
-
-    @pl.when(z > 0)
-    def _():
-        signal({"heads": z - 1})
-
-    @pl.when(z < count - 1)
-    def _():
-        signal({"heads": z + 1})
-
-    pl.semaphore_wait(barrier, 2 + jnp.minimum(z, 1) + jnp.minimum(count - 1 - z, 1))
-
-
 def nearest(count, z, index):
     index = count - 1 - index
     more = jnp.maximum(z, count - 1 - z)
@@ -189,10 +169,15 @@
         def _():
             act(copy(1, {"heads": z + 1}))
 
-    def token_copy(zz, own=False):
+    def token_copy(zz, piece, own=False):
+        rows = pl.ds(piece * row_count // PIECES, row_count // PIECES)
+
         def copy(way, device):
-            source = tokens_ref if own else slab_ref.at[zz]
-            return remote(source, slab_ref.at[zz], token_send.at[way, zz], token_recv.at[zz], device)
+            block = slab_ref.at[zz, rows, :]
+            source = tokens_ref.at[rows, :] if own else block
+            return remote(
+                source, block, token_send.at[way, piece, zz], token_recv.at[piece, zz], device
+            )
 
         return copy
 
@@ -242,7 +227,8 @@
         share_received(zz, across)
         aside(started, zz, across)
 
-    along(started, z, token_copy(z, True))
+    for piece in range(PIECES):
+        along(started, z, token_copy(z, piece, True))
     share_relay(started, z, True)
     for copy in local:
         copy.wait()
@@ -266,9 +252,9 @@
             {"ctx": jnp.minimum(c + 1, 3)},
         )
 
-    def token_relay(zz):
-        token_copy(zz)(0, {"heads": z - 1}).wait_recv()
-        along(started, zz, token_copy(zz))
+    def token_relay(zz, piece):
+        token_copy(zz, piece)(0, {"heads": z - 1}).wait_recv()
+        along(started, zz, token_copy(zz, piece))
 
     def step(index, _):
         zz = nearest(count, z, index)
@@ -277,13 +263,15 @@
         opens = jnp.logical_and(index > 0, jnp.abs(zz - z) != jnp.abs(last - z))
         double = jnp.logical_and(index < count - 1, jnp.abs(after - z) == jnp.abs(zz - z))
 
-        @pl.when(opens)
-        def _():
-            token_relay(zz)
-
-        @pl.when(jnp.logical_and(opens, double))
-        def _():
-            token_relay(after)
+        for piece in range(PIECES):
+
+            @pl.when(opens)
+            def _():
+                token_relay(zz, piece)
+
+            @pl.when(jnp.logical_and(opens, double))
+            def _():
+                token_relay(after, piece)
 
         project(zz)
         alone = jnp.logical_and(index > 0, jnp.logical_not(jnp.logical_and(opens, double)))
@@ -436,7 +424,8 @@
         hidden = hidden_ref[:, first : first + DOT_COLUMNS].astype(jnp.float32)
         normed_ref[:, first : first + DOT_COLUMNS] = (hidden * inverse).astype(normed_ref.dtype)
 
-    along(left, z, token_copy(z, True))
+    for piece in range(PIECES):
+        along(left, z, token_copy(z, piece, True))
     share_along(left, z, True)
     share_relay(left, z, True)
 
@@ -452,7 +441,8 @@
 
         @pl.when(zz != z)
         def _():
-            along(left, zz, token_copy(zz))
+            for piece in range(PIECES):
+                along(left, zz, token_copy(zz, piece))
             share_along(left, zz)
             share_relay(left, zz)
             head_copy(zz).wait_send()
@@ -505,7 +495,7 @@
 
 
 def expert_kernel(
-    count, hidden_ref, own_ref, table_ref, gate_hbm, up_hbm, down_hbm, out_ref,
+    count, weight_copies, hidden_ref, own_ref, table_ref, out_ref,
     rows_ref, part_ref, hid_ref, scale_ref, gate_ref, up_ref, down_ref,
     from_beside, to_across, from_across, line_out, line_in, last_out, last_in,
     local_sem, row_send, row_recv, beside_send, beside_recv, across_send, across_recv,
@@ -516,20 +506,10 @@
     spans, far_rows = span_rows(row_count)
     near_rows = row_count - far_rows
     expert = c * count + z
-    local = [
-        pltpu.make_async_copy(source, target, local_sem.at[index])
-        for index, (source, target) in enumerate(
-            [
-                (gate_hbm, gate_ref),
-                (up_hbm, up_ref),
-                (down_hbm, down_ref),
-                (own_ref, rows_ref.at[z, pl.ds(pl.multiple_of(c * row_count, row_count), row_count), :]),
-            ]
-        )
-    ]
-    for copy in local:
-        copy.start()
-    greet(z, count, beside, across)
+    own_rows = pl.ds(pl.multiple_of(c * row_count, row_count), row_count)
+    own_copy = pltpu.make_async_copy(own_ref, rows_ref.at[z, own_rows, :], local_sem)
+    own_copy.start()
+    local = weight_copies + [own_copy]
 
     def window(cc, span):
         first, size, _ = spans[span]
@@ -834,102 +814,105 @@
     each_place(finish)
 
 
-def attend(tokens, w_out, table, state_in, past_kv, w_qkv):
+def layer_kernel(
+    count, front_size, tokens_ref, share_hbm, table_ref, state_ref, past_hbm, qkv_hbm,
+    gate_hbm, up_hbm, down_hbm, out_ref, hidden_ref, normed_ref, tables_ref, weight_sem, *scratch
+):
+    front, back = scratch[:front_size], scratch[front_size:]
+    weight_copies = [
+        pltpu.make_async_copy(source, target, weight_sem.at[index])
+        for index, (source, target) in enumerate(zip((gate_hbm, up_hbm, down_hbm), back[4:7]))
+    ]
+    for copy in weight_copies:
+        copy.start()
+    attend_kernel(
+        count, tokens_ref, share_hbm, table_ref, state_ref, past_hbm, qkv_hbm,
+        hidden_ref, normed_ref, tables_ref, *front,
+    )
+    expert_kernel(count, weight_copies, hidden_ref, normed_ref, tables_ref, out_ref, *back)
+
+
+def run_layer(tokens, w_out, table, state_in, past_kv, w_qkv, w_gate, w_up, w_down):
     count = lax.axis_size("heads")
     row_count, width = tokens.shape
     slab_rows = count * row_count
+    inner = w_gate.shape[1]
     kind = tokens.dtype
     slots = 4 * count
-    dma = pltpu.SemaphoreType.DMA
-    vmem, anywhere = pl.BlockSpec(memory_space=pltpu.VMEM), pl.BlockSpec(memory_space=pl.ANY)
-    return pl.pallas_call(
-        functools.partial(attend_kernel, count),
-        out_shape=[
-            jax.ShapeDtypeStruct((row_count, width), kind),
-            jax.ShapeDtypeStruct((row_count, width), kind),
-            jax.ShapeDtypeStruct((slots,) + table.shape, table.dtype),
-        ],
-        in_specs=[vmem, anywhere, vmem, vmem, anywhere, anywhere],
-        out_specs=[vmem, vmem, anywhere],
-        scratch_shapes=[
-            pltpu.VMEM((count, row_count, width), kind),
-            pltpu.VMEM((width, 3 * HDIM), kind),
-            pltpu.VMEM((count * HDIM, width), kind),
-            pltpu.VMEM((slab_rows, HDIM), kind),
-            pltpu.VMEM((2, slab_rows, HDIM), kind),
-            pltpu.VMEM((2, WINDOW, HDIM), kind),
-            pltpu.VMEM((slab_rows, slab_rows), jnp.float32),
-            pltpu.VMEM((slab_rows, HDIM), jnp.float32),
-            pltpu.VMEM((HDIM, HDIM), kind),
-            pltpu.VMEM((4, HDIM, HDIM), kind),
-            pltpu.VMEM((count, row_count, HDIM), kind),
-            pltpu.VMEM((row_count, count * HDIM), kind),
-            dma((7,)),
-            dma((2, count)),
-            dma((count,)),
-            dma((2, 4, slots)),
-            dma((2, slots)),
-            dma((count,)),
-            dma((count,)),
-            dma((3,)),
-            dma((4,)),
-            dma((count,)),
-            dma((count,)),
-        ],
-        compiler_params=pltpu.CompilerParams(
-            collective_id=2, has_side_effects=True, vmem_limit_bytes=FRONT_BYTES
-        ),
-        name="attend",
-    )(tokens, w_out, table, state_in, past_kv, w_qkv)
-
-
-def run_experts(hidden, normed, tables, w_gate, w_up, w_down):
-    count = lax.axis_size("heads")
-    row_count, width = normed.shape
-    inner = w_gate.shape[1]
     far_rows = span_rows(row_count)[1]
     near_rows = row_count - far_rows
     cuts = len(SPANS)
     dma = pltpu.SemaphoreType.DMA
-    kind = normed.dtype
     vmem, anywhere = pl.BlockSpec(memory_space=pltpu.VMEM), pl.BlockSpec(memory_space=pl.ANY)
+    shared = [
+        pltpu.VMEM((row_count, width), kind),
+        pltpu.VMEM((row_count, width), kind),
+        pltpu.VMEM((slots,) + table.shape, table.dtype),
+        dma((3,)),
+    ]
+    front = [
+        pltpu.VMEM((count, row_count, width), kind),
+        pltpu.VMEM((width, 3 * HDIM), kind),
+        pltpu.VMEM((count * HDIM, width), kind),
+        pltpu.VMEM((slab_rows, HDIM), kind),
+        pltpu.VMEM((2, slab_rows, HDIM), kind),
+        pltpu.VMEM((2, WINDOW, HDIM), kind),
+        pltpu.VMEM((slab_rows, slab_rows), jnp.float32),
+        pltpu.VMEM((slab_rows, HDIM), jnp.float32),
+        pltpu.VMEM((HDIM, HDIM), kind),
+        pltpu.VMEM((4, HDIM, HDIM), kind),
+        pltpu.VMEM((count, row_count, HDIM), kind),
+        pltpu.VMEM((row_count, count * HDIM), kind),
+        dma((7,)),
+        dma((2, PIECES, count)),
+        dma((PIECES, count)),
+        dma((2, 4, slots)),
+        dma((2, slots)),
+        dma((count,)),
+        dma((count,)),
+        dma((3,)),
+        dma((4,)),
+        dma((count,)),
+        dma((count,)),
+    ]
+    back = [
+        pltpu.VMEM((count, 4 * row_count, width), kind),
+        pltpu.VMEM((count, 4 * row_count, width), kind),
+        pltpu.VMEM((2 * row_count, inner), kind),
+        pltpu.VMEM((2 * row_count, HDIM), jnp.float32),
+        pltpu.VMEM(w_gate.shape, kind),
+        pltpu.VMEM(w_up.shape, kind),
+        pltpu.VMEM(w_down.shape, kind),
+        pltpu.VMEM((2, count, row_count, width), kind),
+        pltpu.VMEM((count, near_rows, width), kind),
+        pltpu.VMEM((count, near_rows, width), kind),
+        pltpu.VMEM((count, row_count + far_rows, width), kind),
+        pltpu.VMEM((2, count, row_count + far_rows, width), kind),
+        pltpu.VMEM((far_rows, width), kind),
+        pltpu.VMEM((far_rows, width), kind),
+        dma(()),
+        dma((4, cuts, 4 * count)),
+        dma((cuts, 4 * count)),
+        dma((2, count)),
+        dma((2, count)),
+        dma((cuts, count)),
+        dma((cuts, count)),
+        dma((2 * cuts, count)),
+        dma((2 * cuts, 2, count)),
+        dma((cuts,)),
+        dma((cuts,)),
+    ]
     return pl.pallas_call(
-        functools.partial(expert_kernel, count),
+        functools.partial(layer_kernel, count, len(front)),
         out_shape=jax.ShapeDtypeStruct((row_count, width), kind),
-        in_specs=[vmem] * 3 + [anywhere] * 3,
+        in_specs=[vmem, anywhere, vmem, vmem] + [anywhere] * 5,
         out_specs=vmem,
-        scratch_shapes=[
-            pltpu.VMEM((count, 4 * row_count, width), kind),
-            pltpu.VMEM((count, 4 * row_count, width), kind),
-            pltpu.VMEM((2 * row_count, inner), kind),
-            pltpu.VMEM((2 * row_count, HDIM), jnp.float32),
-            pltpu.VMEM(w_gate.shape, kind),
-            pltpu.VMEM(w_up.shape, kind),
-            pltpu.VMEM(w_down.shape, kind),
-            pltpu.VMEM((2, count, row_count, width), kind),
-            pltpu.VMEM((count, near_rows, width), kind),
-            pltpu.VMEM((count, near_rows, width), kind),
-            pltpu.VMEM((count, row_count + far_rows, width), kind),
-            pltpu.VMEM((2, count, row_count + far_rows, width), kind),
-            pltpu.VMEM((far_rows, width), kind),
-            pltpu.VMEM((far_rows, width), kind),
-            dma((4,)),
-            dma((4, cuts, 4 * count)),
-            dma((cuts, 4 * count)),
-            dma((2, count)),
-            dma((2, count)),
-            dma((cuts, count)),
-            dma((cuts, count)),
-            dma((2 * cuts, count)),
-            dma((2 * cuts, 2, count)),
-            dma((cuts,)),
-            dma((cuts,)),
-        ],
+        scratch_shapes=shared + front + back,
         compiler_params=pltpu.CompilerParams(
             collective_id=0, has_side_effects=True, vmem_limit_bytes=VMEM_BYTES
         ),
-        name="run_experts",
-    )(hidden, normed, tables, w_gate, w_up, w_down)
+        name="run_layer",
+    )(tokens, w_out, table, state_in, past_kv, w_qkv, w_gate, w_up, w_down)
 
 
 def expert_table(expert_ids, gate_weights, expert_count):
@@ -961,10 +944,10 @@
     )
     if dense:
         table = expert_table(expert_ids, gate_weights, expert_count)
-        hidden_state, normed, tables = attend(
-            tokens, w_out, table, state_in[0], past_kv, jnp.transpose(w_qkv, (1, 0, 2))
-        )
-        return run_experts(hidden_state, normed, tables, w_gate[0], w_up[0], w_down[0])
+        return run_layer(
+            tokens, w_out, table, state_in[0], past_kv, jnp.transpose(w_qkv, (1, 0, 2)),
+            w_gate[0], w_up[0], w_down[0],
+        )
     slab, w_rows = [
         lax.all_gather(value, "heads", axis=0, tiled=True) for value in (tokens, w_out)
     ]

time: 159 us -> 154 us (0.969)
  Pallas kernels: 155 us -> 151 us
    pallas_call x2 -> x1, Pallas kernels: 155 us -> 151 us  [run_layer(): pl.pallas_call(functools.partial(layer_kernel, count, len(front)), out_sh...]
where the time goes in v5:
time: 154 us
  Pallas kernels  151 us (98%)
  local copies, waits for them, and re-layouts  1.88 us (1%)
    pallas_call x1, Pallas kernels, run_layer(): pl.pallas_call(functools.partial(layer_kernel, count, len(front)), out_sh...  151 us

profile of v5, /device:TPU:0, one launch (start us, length us, event | category | flops | bytes accessed | tf_op | source)
XLA Modules:
  0.0 153.8 jit_solution(15734205237672711585)
XLA Ops:
  0.0 1.3 select_reduce_fusion
  1.3 150.6 %run_layer.1 = bf16[128,2048]{1,0:T(8,128)(2,1)} custom-call(bf16[128,2048]{1,0:T(8,128)(2,1)} %tokens_ref.1, bf16[128,2048]{1,0:T(8,128)(2,1)} %share_hbm.1, f32[16,128]{1,0:T(8,128)} %bitcast.11, f32[128,128]{1,0:T(8,128)} %bitcast.10, bf16[2,512,128]{2,1,0:T(8,128)(2,1)} %past_hbm.1, bf16[3,2048,128]{2,1,0:T(8,128)(2,1)} %bitcast.9, ...), custom_call_target="tpu_custom_call" | custom-call | tf_op jit(solution)/shard_map/run_layer/pallas_call | solution.py:905
  151.9 1.9 %copy.14 = bf16[128,2048]{1,0:T(8,128)(2,1)} copy(bf16[128,2048]{1,0:T(8,128)(2,1)} %run_layer.1) | data formatting | bytes 1048576

commit v6 on v5

--- a/solution.py
+++ b/solution.py
@@ -411,7 +411,7 @@
     def out_tile(index, total):
         columns = pl.ds(pl.multiple_of(index * DOT_COLUMNS, DOT_COLUMNS), DOT_COLUMNS)
         attn = jnp.dot(heads_in[...], w_ref[:, columns], preferred_element_type=jnp.float32)
-        hidden = (tokens_ref[:, columns].astype(jnp.float32) + attn).astype(hidden_ref.dtype)
+        hidden = (slab_ref[z, :, columns].astype(jnp.float32) + attn).astype(hidden_ref.dtype)
         hidden_ref[:, columns] = hidden
         hidden = hidden.astype(jnp.float32)
         return total + jnp.sum(hidden * hidden, axis=-1, keepdims=True)
@@ -815,8 +815,9 @@
 
 
 def layer_kernel(
-    count, front_size, tokens_ref, share_hbm, table_ref, state_ref, past_hbm, qkv_hbm,
-    gate_hbm, up_hbm, down_hbm, out_ref, hidden_ref, normed_ref, tables_ref, weight_sem, *scratch
+    count, front_size, tokens_ref, share_hbm, ids_ref, gates_ref, state_ref, past_hbm, qkv_hbm,
+    gate_hbm, up_hbm, down_hbm, out_ref, hidden_ref, normed_ref, table_ref, tables_ref, weight_sem,
+    *scratch
 ):
     front, back = scratch[:front_size], scratch[front_size:]
     weight_copies = [
@@ -825,6 +826,12 @@
     ]
     for copy in weight_copies:
         copy.start()
+    experts = lax.broadcasted_iota(jnp.int32, table_ref.shape, 0)
+    table = jnp.zeros(table_ref.shape, table_ref.dtype)
+    for pick in range(ids_ref.shape[0]):
+        chosen = ids_ref[pick : pick + 1, :] == experts
+        table = table + jnp.where(chosen, gates_ref[pick : pick + 1, :], 0.0)
+    table_ref[...] = table
     attend_kernel(
         count, tokens_ref, share_hbm, table_ref, state_ref, past_hbm, qkv_hbm,
         hidden_ref, normed_ref, tables_ref, *front,
@@ -832,7 +839,7 @@
     expert_kernel(count, weight_copies, hidden_ref, normed_ref, tables_ref, out_ref, *back)
 
 
-def run_layer(tokens, w_out, table, state_in, past_kv, w_qkv, w_gate, w_up, w_down):
+def run_layer(tokens, w_out, ids, gates, state_in, past_kv, w_qkv, w_gate, w_up, w_down):
     count = lax.axis_size("heads")
     row_count, width = tokens.shape
     slab_rows = count * row_count
@@ -847,7 +854,8 @@
     shared = [
         pltpu.VMEM((row_count, width), kind),
         pltpu.VMEM((row_count, width), kind),
-        pltpu.VMEM((slots,) + table.shape, table.dtype),
+        pltpu.VMEM((slots, row_count), gates.dtype),
+        pltpu.VMEM((slots, slots, row_count), gates.dtype),
         dma((3,)),
     ]
     front = [
@@ -905,19 +913,14 @@
     return pl.pallas_call(
         functools.partial(layer_kernel, count, len(front)),
         out_shape=jax.ShapeDtypeStruct((row_count, width), kind),
-        in_specs=[vmem, anywhere, vmem, vmem] + [anywhere] * 5,
+        in_specs=[anywhere] * 2 + [vmem] * 3 + [anywhere] * 5,
         out_specs=vmem,
         scratch_shapes=shared + front + back,
         compiler_params=pltpu.CompilerParams(
             collective_id=0, has_side_effects=True, vmem_limit_bytes=VMEM_BYTES
         ),
         name="run_layer",
-    )(tokens, w_out, table, state_in, past_kv, w_qkv, w_gate, w_up, w_down)
-
-
-def expert_table(expert_ids, gate_weights, expert_count):
-    chosen = expert_ids[:, :, None] == jnp.arange(expert_count, dtype=jnp.int32)
-    return jnp.sum(jnp.where(chosen, gate_weights[:, :, None], 0.0), axis=1).T
+    )(tokens, w_out, ids, gates, state_in, past_kv, w_qkv, w_gate, w_up, w_down)
 
 
 def on_device(
@@ -943,10 +946,9 @@
         and row_count * devices <= expert_count * capacity
     )
     if dense:
-        table = expert_table(expert_ids, gate_weights, expert_count)
         return run_layer(
-            tokens, w_out, table, state_in[0], past_kv, jnp.transpose(w_qkv, (1, 0, 2)),
-            w_gate[0], w_up[0], w_down[0],
+            tokens, w_out, expert_ids.T, gate_weights.T, state_in[0], past_kv,
+            jnp.transpose(w_qkv, (1, 0, 2)), w_gate[0], w_up[0], w_down[0],
         )
     slab, w_rows = [
         lax.all_gather(value, "heads", axis=0, tiled=True) for value in (tokens, w_out)

time: 154 us -> 153 us (level)
  no operation moved by 1% of the time
where the time goes in v6:
time: 153 us; the launch traced here: 152 us
  Pallas kernels  151 us (99%)
  local copies, waits for them, and re-layouts  1.88 us (1%)
    pallas_call x1, Pallas kernels, run_layer(): pl.pallas_call(functools.partial(layer_kernel, count, len(front)), out_sh...  151 us

profile of v6, /device:TPU:0, one launch (start us, length us, event | category | flops | bytes accessed | tf_op | source)
XLA Modules:
  0.0 152.5 jit_solution(7571364518512042304)
XLA Ops:
  0.0 150.6 %run_layer.1 = bf16[128,2048]{1,0:T(8,128)(2,1)} custom-call(bf16[128,2048]{1,0:T(8,128)(2,1)} %tokens_ref.1, bf16[128,2048]{1,0:T(8,128)(2,1)} %share_hbm.1, s32[8,128]{1,0:T(8,128)} %bitcast.12, f32[8,128]{1,0:T(8,128)} %bitcast.13, f32[128,128]{1,0:T(8,128)} %bitcast.11, bf16[2,512,128]{2,1,0:T(8,128)(2,1)} %past_hbm.1, bf16[3,2048,128]{2,1,0:T(8,128)(2,1)} %bitcast.10, ...), custom_call_target="tpu_custom_call" | custom-call | tf_op jit(solution)/shard_map/run_layer/pallas_call | solution.py:913
  150.6 1.9 %copy.12 = bf16[128,2048]{1,0:T(8,128)(2,1)} copy(bf16[128,2048]{1,0:T(8,128)(2,1)} %run_layer.1) | data formatting | bytes 1048576

commit v7 on v6

--- a/solution.py
+++ b/solution.py
@@ -37,7 +37,7 @@
 VMEM_BYTES = 62 * 1024 * 1024
 ADD_ROWS = 16
 PIECES = 2
-DOT_COLUMNS = 512
+DOT_COLUMNS = 1024
 HID_COLUMNS = 256
 SPANS = ((32, 0), (32, 0), (32, 0), (32, 1))
 OWN_LINE, OWN_OVER, OWN_ASIDE, LOAD, ROWS, CROSS = range(6)

time: 153 us -> 152 us (level)
  no operation moved by 1% of the time
where the time goes in v7:
time: 152 us
  Pallas kernels  150 us (99%)
  local copies, waits for them, and re-layouts  1.88 us (1%)
    pallas_call x1, Pallas kernels, run_layer(): pl.pallas_call(functools.partial(layer_kernel, count, len(front)), out_sh...  150 us

profile of v7, /device:TPU:0, one launch (start us, length us, event | category | flops | bytes accessed | tf_op | source)
XLA Modules:
  0.0 151.6 jit_solution(6898308416942677638)
XLA Ops:
  0.0 149.7 %run_layer.1 = bf16[128,2048]{1,0:T(8,128)(2,1)} custom-call(bf16[128,2048]{1,0:T(8,128)(2,1)} %tokens_ref.1, bf16[128,2048]{1,0:T(8,128)(2,1)} %share_hbm.1, s32[8,128]{1,0:T(8,128)} %bitcast.12, f32[8,128]{1,0:T(8,128)} %bitcast.13, f32[128,128]{1,0:T(8,128)} %bitcast.11, bf16[2,512,128]{2,1,0:T(8,128)(2,1)} %past_hbm.1, bf16[3,2048,128]{2,1,0:T(8,128)(2,1)} %bitcast.10, ...), custom_call_target="tpu_custom_call" | custom-call | tf_op jit(solution)/shard_map/run_layer/pallas_call | solution.py:913
  149.8 1.9 %copy.12 = bf16[128,2048]{1,0:T(8,128)(2,1)} copy(bf16[128,2048]{1,0:T(8,128)(2,1)} %run_layer.1) | data formatting | bytes 1048576
